TPU v7x, 512 devices: a whole 4x8x8 slice. The times are simulated.
512 devices in a mesh: src: 32 (over x, y), col: 16 (over z, core).
Axes of the slice: x: 4, y: 8, z: 8, core: 2. Of those that a mesh axis runs over, the one named last changes fastest.
Arguments:
- perambulator: bfloat16 [32, 16, 2, 768, 768], P('src', None, None, 'col'), may hold values from -0.15625 to 0.15625
- elementals: bfloat16 [16, 4, 2, 192, 192], P('col'), may hold values from -0.3125 to 0.3125
- sink_block: bfloat16 [2, 768, 128], replicated, may hold values from -6 to 6
- gamma_spin: float32 [2, 4, 4], replicated, may hold values from -2.5 to 2.5
- graph_lists: int32 [32, 6, 3], P('src'), may hold values from 0 to 31, as said below
- diagram_counts: int32 [32], P('src'), may hold values from 1 to 6, as said below
- source_ids: int32 [32], P('src'), may hold values from 0 to 3
Outputs:
- contraction: float32 [32, 16, 6, 2, 128, 128], P('src', 'col')
Inputs may be any that keep to these rules, and one draw needn't show every extreme that they name: `graph_lists`: both senders of a slot of receiver t lie within 2 of t; in slot 0 the first sender is t - 2 and the second t + 2 where these exist (else t + 2, t - 2); the third entry is below 4; every slot holds valid entries. `diagram_counts`: at least one source time has exactly 6 live slots.
All inputs are finite; a program needn't handle non-finite values.
Results may differ from a plain program's by a relative error of at most 0.018.
Values may be sent and summed in bfloat16 or wider, within the bound.
No kernel may reach another device: no remote copies, remote signals or barrier semaphores. Data moves between devices by JAX's collectives and lax.ppermute only.
A program may use at most 64 MiB of HBM per device.

v0:
```python
import functools

import jax
import jax.numpy as jnp
from jax import lax
from jax.experimental import pallas as pl
from jax.experimental.pallas import tpu as pltpu
from jax.sharding import PartitionSpec as P

DT = 2
BF = jnp.bfloat16
F32 = jnp.float32


def shifted(shard, axis, by):
    count = lax.axis_size(axis)
    pairs = [(i, i + by) for i in range(count) if 0 <= i + by < count]
    return lax.ppermute(shard, axis, pairs)


def dot(left, right):
    return jnp.dot(left, right, preferred_element_type=F32)


def mix(values_r, values_i, g_r, g_i):
    out_r = g_r[0] * values_r[0] - g_i[0] * values_i[0]
    out_i = g_r[0] * values_i[0] + g_i[0] * values_r[0]
    for s in range(1, 4):
        out_r += g_r[s] * values_r[s] - g_i[s] * values_i[s]
        out_i += g_r[s] * values_i[s] + g_i[s] * values_r[s]
    return out_r, out_i


def tau_times(rows, tau_r, tau_i):
    half = rows.shape[0] // 2
    by_r = dot(rows, tau_r)
    by_i = dot(rows, tau_i)
    return by_r[:half] - by_i[half:], by_r[half:] + by_i[:half]


def dress_kernel(ident, gamma, pieces, sink_rows, forward, out, split, mixed):
    chunks, _, depth, ndim = pieces.shape
    width = out.shape[2]
    nev = ndim // 4
    tau_r = pieces[:, 0].reshape(chunks * depth, ndim)
    tau_i = pieces[:, 1].reshape(chunks * depth, ndim)
    prop_r, prop_i = tau_times(sink_rows[...], tau_r, tau_i)
    split[0] = prop_r.astype(BF).astype(F32).T
    split[1] = prop_i.astype(BF).astype(F32).T
    part_r = [split[0, pl.ds(s, nev, stride=4), :] for s in range(4)]
    part_i = [split[1, pl.ds(s, nev, stride=4), :] for s in range(4)]
    for s in range(4):
        g_r = [gamma[0, s, q] for q in range(4)]
        g_i = [gamma[1, s, q] for q in range(4)]
        m_r, m_i = mix(part_r, part_i, g_r, g_i)
        at_r = slice(s * width, (s + 1) * width)
        at_i = slice((4 + s) * width, (5 + s) * width)
        mixed[:nev, at_r] = m_r.astype(BF)
        mixed[:nev, at_i] = m_i.astype(BF)
        mixed[nev:, at_r] = (-m_i).astype(BF)
        mixed[nev:, at_i] = m_r.astype(BF)
    done = dot(forward[ident[0]], mixed[...])
    for c in range(2):
        for s in range(4):
            split[c, pl.ds(s, nev, stride=4), :] = done[:, (4 * c + s) * width : (4 * c + s + 1) * width]
    out[...] = split[...].astype(BF)


def diagrams_kernel(
    lists, count, position, gamma, pieces, d0, d1, d2, d3, d4, backward, out, wide, mixed, split, column
):
    chunks, _, depth, ndim = pieces.shape
    blocks = (d0, d1, d2, d3, d4)
    width = d0.shape[2]
    nev = ndim // 4
    tau_r = pieces[:, 0].reshape(chunks * depth, ndim)
    tau_i = pieces[:, 1].reshape(chunks * depth, ndim)
    for d, block in enumerate(blocks):
        rows = jnp.concatenate([block[0].T, block[1].T], axis=0)
        w_r, w_i = tau_times(rows, tau_r, tau_i)
        wide[d, :, :ndim] = w_r.astype(BF)
        wide[d, :, ndim:] = w_i.astype(BF)
        split[...] = block[...].astype(F32)
        part_r = [split[0, pl.ds(s, nev, stride=4), :] for s in range(4)]
        part_i = [split[1, pl.ds(s, nev, stride=4), :] for s in range(4)]
        for s in range(4):
            g_r = [gamma[0, q, s] for q in range(4)]
            g_i = [-gamma[1, q, s] for q in range(4)]
            m_r, m_i = mix(part_r, part_i, g_r, g_i)
            at_r = slice(s * width, (s + 1) * width)
            at_i = slice((4 + s) * width, (5 + s) * width)
            mixed[d, :nev, at_r] = m_r.astype(BF)
            mixed[d, :nev, at_i] = m_i.astype(BF)
            mixed[d, nev:, at_r] = m_i.astype(BF)
            mixed[d, nev:, at_i] = (-m_r).astype(BF)
    scale = (2.0 * ndim) ** (-0.5)
    offset = DT - position[0]
    for k in range(out.shape[0]):
        first = lists[k, 0] + offset
        second = lists[k, 1] + offset
        done = dot(backward[lists[k, 2]], mixed[first])
        for c in range(2):
            for s in range(4):
                at = slice((4 * c + s) * width, (4 * c + s + 1) * width)
                split[c, pl.ds(s, nev, stride=4), :] = done[:, at]
        u_r = split[0].astype(BF)
        u_i = split[1].astype(BF)
        column[:ndim, :width] = u_r
        column[:ndim, width:] = u_i
        column[ndim:, :width] = u_i
        column[ndim:, width:] = -u_r
        result = dot(wide[second], column[...]) * scale
        result = jnp.where(k < count[0], result, 0.0)
        out[k, 0] = result[:, :width]
        out[k, 1] = result[:, width:]


def per_device(
    perambulator, elementals, sink_block, gamma_spin, graph_lists, diagram_counts, source_ids
):
    ndim, width = sink_block.shape[1:]
    slots = graph_lists.shape[1]
    nev = elementals.shape[3]
    row_block = lax.all_to_all(perambulator, "col", split_axis=1, concat_axis=1, tiled=True)
    pieces = row_block[0]
    table = elementals[0]
    sink_rows = jnp.swapaxes(sink_block, 1, 2).reshape(2 * width, ndim)
    forward = jnp.concatenate([table[:, 0], table[:, 1]], axis=2)
    backward = jnp.concatenate(
        [jnp.swapaxes(table[:, 0], 1, 2), jnp.swapaxes(table[:, 1], 1, 2)], axis=2
    )
    smem = pl.BlockSpec(memory_space=pltpu.SMEM)
    vmem = pl.BlockSpec(memory_space=pltpu.VMEM)
    dressed = pl.pallas_call(
        dress_kernel,
        out_shape=jax.ShapeDtypeStruct((2, ndim, width), BF),
        in_specs=[smem, smem, vmem, vmem, vmem],
        out_specs=vmem,
        scratch_shapes=[
            pltpu.VMEM((2, ndim, width), F32),
            pltpu.VMEM((2 * nev, 8 * width), BF),
        ],
        name="dress",
    )(source_ids, gamma_spin, pieces, sink_rows, forward)
    blocks = [dressed if d == DT else shifted(dressed, "src", DT - d) for d in range(2 * DT + 1)]
    position = lax.axis_index("src").astype(jnp.int32).reshape(1)
    totals = pl.pallas_call(
        diagrams_kernel,
        out_shape=jax.ShapeDtypeStruct((slots, 2, width, width), F32),
        in_specs=[smem] * 4 + [vmem] * 7,
        out_specs=vmem,
        scratch_shapes=[
            pltpu.VMEM((2 * DT + 1, width, 2 * ndim), BF),
            pltpu.VMEM((2 * DT + 1, 2 * nev, 8 * width), BF),
            pltpu.VMEM((2, ndim, width), F32),
            pltpu.VMEM((2 * ndim, 2 * width), BF),
        ],
        name="diagrams",
    )(graph_lists[0], diagram_counts, position, gamma_spin, pieces, *blocks, backward)
    return totals[None, None]


def solution(mesh):
    in_specs = (
        P("src", None, None, "col", None),
        P("col", None, None, None, None),
        P(),
        P(),
        P("src", None, None),
        P("src"),
        P("src"),
    )
    out_specs = P("src", "col", None, None, None, None)
    return jax.shard_map(
        per_device, mesh=mesh, in_specs=in_specs, out_specs=out_specs, check_vma=False
    )
```

profile of v0, /device:TPU:6, one launch (start us, length us, event | category | flops | bytes accessed | tf_op | source)
XLA Modules:
  0.0 126.7 jit_solution(6322512259840337248)
XLA Ops:
  0.0 0.0 copy-start.6
  0.0 10.6 %all-to-all-start = ((bf16[1,16,2,48,768]{4,3,2,0,1:T(8,128)(2,1)}), bf16[1,16,2,48,768]{4,3,2,0,1:T(8,128)(2,1)S(1)}, u32[]{:S(2)}, u32[]{:S(2)}) async-start(bf16[1,16,2,48,768]{4,3,2,0,1:T(8,128)(2,1)} %bitcast.21), calls=%async_computation | async-start | bytes 4718592 | tf_op jit(solution)/shard_map/all_to_all | solution.py:124
  11.2 0.0 copy-done.6
  11.2 0.9 copy.13
  12.1 1.5 %copy.14 = bf16[1,4,2,192,192]{3,4,1,2,0:T(8,128)(2,1)S(1)} copy(bf16[1,4,2,192,192]{4,3,2,1,0:T(8,128)(2,1)} %param.8) | data formatting | bytes 1179648 | tf_op args[1]
  13.6 0.9 slice_bitcast_fusion.2
  14.5 0.1 pad_maximum_fusion
  14.7 1.1 copy.15.forward
  15.8 49.7 %all-to-all-done = bf16[1,16,2,48,768]{4,3,2,0,1:T(8,128)(2,1)S(1)} async-done(((bf16[1,16,2,48,768]{4,3,2,0,1:T(8,128)(2,1)}), bf16[1,16,2,48,768]{4,3,2,0,1:T(8,128)(2,1)S(1)}, u32[]{:S(2)}, u32[]{:S(2)}) %all-to-all-start) | async-done | bytes 2359328 | tf_op jit(solution)/shard_map/all_to_all | solution.py:124
  65.5 0.0 copy-start
  65.5 1.4 %copy-done = bf16[1,16,2,48,768]{4,3,2,0,1:T(8,128)(2,1)} copy-done((bf16[1,16,2,48,768]{4,3,2,0,1:T(8,128)(2,1)}, bf16[1,16,2,48,768]{4,3,2,0,1:T(8,128)(2,1)S(1)}, u32[]{:S(2)}) %copy-start) | copy-done | bytes 2359320
  66.9 0.0 copy-start.7
  67.0 0.0 copy-start.1
  67.0 4.6 %dress.1.d2 = bf16[2,768,128]{2,1,0:T(8,128)(2,1)} custom-call(s32[1]{0:T(128)S(6)} %copy.19.ident, f32[2,4,4]{2,1,0:T(4,128)} %gamma.3, bf16[16,2,48,768]{3,2,1,0:T(8,128)(2,1)} %bitcast.18, bf16[256,768]{1,0:T(8,128)(2,1)} %bitcast.22, bf16[4,192,384]{2,1,0:T(8,128)(2,1)} %copy.15.forward), custom_call_target="tpu_custom_call" | custom-call | tf_op jit(solution)/shard_map/dress/pallas_call | solution.py:134
  71.5 6.4 %collective-permute-start.3 = (bf16[2,768,128]{2,1,0:T(8,128)(2,1)}, bf16[2,768,128]{2,1,0:T(8,128)(2,1)S(1)}, u32[]{:S(2)}, u32[]{:S(2)}) collective-permute-start(bf16[2,768,128]{2,1,0:T(8,128)(2,1)} %dress.1.d2), channel_id=1, source_target_pairs={{32,0},{48,16},{64,32},{80,48},{96,64},{112,80},{128,96},{144,112}... | collective-permute-start | bytes 1179656 | tf_op jit(solution)/shard_map/ppermute | solution.py:18
  77.9 3.3 %collective-permute-start.2 = (bf16[2,768,128]{2,1,0:T(8,128)(2,1)}, bf16[2,768,128]{2,1,0:T(8,128)(2,1)S(1)}, u32[]{:S(2)}, u32[]{:S(2)}) collective-permute-start(bf16[2,768,128]{2,1,0:T(8,128)(2,1)} %dress.1.d2), channel_id=1, source_target_pairs={{16,0},{32,16},{48,32},{64,48},{80,64},{96,80},{112,96},{128,112},... | collective-permute-start | bytes 1179656 | tf_op jit(solution)/shard_map/ppermute | solution.py:18
  81.2 2.6 %collective-permute-start.1 = (bf16[2,768,128]{2,1,0:T(8,128)(2,1)}, bf16[2,768,128]{2,1,0:T(8,128)(2,1)S(1)}, u32[]{:S(2)}, u32[]{:S(2)}) collective-permute-start(bf16[2,768,128]{2,1,0:T(8,128)(2,1)} %dress.1.d2), channel_id=1, source_target_pairs={{0,16},{16,32},{32,48},{48,64},{64,80},{80,96},{96,112},{112,128},... | collective-permute-start | bytes 1179656 | tf_op jit(solution)/shard_map/ppermute | solution.py:18
  83.8 2.2 %collective-permute-start = (bf16[2,768,128]{2,1,0:T(8,128)(2,1)}, bf16[2,768,128]{2,1,0:T(8,128)(2,1)S(1)}, u32[]{:S(2)}, u32[]{:S(2)}) collective-permute-start(bf16[2,768,128]{2,1,0:T(8,128)(2,1)} %dress.1.d2), channel_id=1, source_target_pairs={{0,32},{16,48},{32,64},{48,80},{64,96},{80,112},{96,128},{112,144}... | collective-permute-start | bytes 1179656 | tf_op jit(solution)/shard_map/ppermute | solution.py:18
  86.7 0.0 copy-done.7
  86.7 0.7 copy.17
  87.4 0.0 copy-done.1
  87.4 1.0 pad_maximum_fusion.1.backward
  88.4 6.5 %collective-permute-done.3.d4 = bf16[2,768,128]{2,1,0:T(8,128)(2,1)S(1)} collective-permute-done((bf16[2,768,128]{2,1,0:T(8,128)(2,1)}, bf16[2,768,128]{2,1,0:T(8,128)(2,1)S(1)}, u32[]{:S(2)}, u32[]{:S(2)}) %collective-permute-start.3) | collective-permute-done | bytes 393248 | tf_op jit(solution)/shard_map/ppermute | solution.py:18
  94.9 0.0 copy-start.2
  94.9 8.5 %collective-permute-done.2.d3 = bf16[2,768,128]{2,1,0:T(8,128)(2,1)S(1)} collective-permute-done((bf16[2,768,128]{2,1,0:T(8,128)(2,1)}, bf16[2,768,128]{2,1,0:T(8,128)(2,1)S(1)}, u32[]{:S(2)}, u32[]{:S(2)}) %collective-permute-start.2) | collective-permute-done | bytes 393248 | tf_op jit(solution)/shard_map/ppermute | solution.py:18
  103.4 0.0 copy-start.3
  103.4 2.4 %collective-permute-done.1.d1 = bf16[2,768,128]{2,1,0:T(8,128)(2,1)S(1)} collective-permute-done((bf16[2,768,128]{2,1,0:T(8,128)(2,1)}, bf16[2,768,128]{2,1,0:T(8,128)(2,1)S(1)}, u32[]{:S(2)}, u32[]{:S(2)}) %collective-permute-start.1) | collective-permute-done | bytes 393248 | tf_op jit(solution)/shard_map/ppermute | solution.py:18
  105.8 0.0 copy-start.4
  105.8 5.4 %collective-permute-done.d0 = bf16[2,768,128]{2,1,0:T(8,128)(2,1)S(1)} collective-permute-done((bf16[2,768,128]{2,1,0:T(8,128)(2,1)}, bf16[2,768,128]{2,1,0:T(8,128)(2,1)S(1)}, u32[]{:S(2)}, u32[]{:S(2)}) %collective-permute-start) | collective-permute-done | bytes 393248 | tf_op jit(solution)/shard_map/ppermute | solution.py:18
  111.2 0.0 copy-start.5
  111.2 0.0 copy-done.2
  111.2 0.0 copy-done.3
  111.2 0.0 copy-done.4
  111.2 0.7 copy-done.5
  111.9 14.8 %diagrams.1 = f32[6,2,128,128]{3,2,1,0:T(8,128)} custom-call(s32[6,3]{1,0:T(8,128)} %bitcast.24, s32[1]{0:T(128)S(6)} %copy.18.count, s32[1]{0:T(128)} %bitcast.1.position, f32[2,4,4]{2,1,0:T(4,128)} %gamma.3, bf16[16,2,48,768]{3,2,1,0:T(8,128)(2,1)} %bitcast.19, bf16[2,768,128]{2,1,0:T(8,128)(2,1)} %copy-done.5, bf16[2,768,128]{2,1,0:T(8,128)(2,1)} %copy-done.4, ...), custom_call_target="tpu_custom_call" | custom-call | tf_op jit(solution)/shard_map/diagrams/pallas_call | solution.py:147
Async XLA Ops:
  0.0 11.2 %copy-start.6 = (bf16[2,768,128]{2,1,0:T(8,128)(2,1)S(1)}, bf16[2,768,128]{2,1,0:T(8,128)(2,1)}, u32[]{:S(2)}) copy-start(bf16[2,768,128]{2,1,0:T(8,128)(2,1)} %param.9) | copy-start | bytes 1179652
  0.0 65.5 %all-to-all-start = ((bf16[1,16,2,48,768]{4,3,2,0,1:T(8,128)(2,1)}), bf16[1,16,2,48,768]{4,3,2,0,1:T(8,128)(2,1)S(1)}, u32[]{:S(2)}, u32[]{:S(2)}) async-start(bf16[1,16,2,48,768]{4,3,2,0,1:T(8,128)(2,1)} %bitcast.21), calls=%async_computation | async-start | bytes 4718592 | tf_op jit(solution)/shard_map/all_to_all | solution.py:124
  65.5 1.4 %copy-start = (bf16[1,16,2,48,768]{4,3,2,0,1:T(8,128)(2,1)}, bf16[1,16,2,48,768]{4,3,2,0,1:T(8,128)(2,1)S(1)}, u32[]{:S(2)}) copy-start(bf16[1,16,2,48,768]{4,3,2,0,1:T(8,128)(2,1)S(1)} %all-to-all-done) | copy-start | bytes 7077892
  66.9 19.7 %copy-start.7 = (s32[1,6,3]{1,0,2:T(1,128)S(1)}, s32[1,6,3]{1,0,2:T(1,128)}, u32[]{:S(2)}) copy-start(s32[1,6,3]{1,0,2:T(1,128)} %param.11) | copy-start | bytes 220
  67.0 20.4 %copy-start.1 = (bf16[4,192,192]{2,1,0:T(8,128)(2,1)S(1)}, bf16[4,192,192]{2,1,0:T(8,128)(2,1)}, u32[]{:S(2)}) copy-start(bf16[4,192,192]{2,1,0:T(8,128)(2,1)} %get-tuple-element.6) | copy-start | bytes 884740
  71.5 23.4 %collective-permute-start.3 = (bf16[2,768,128]{2,1,0:T(8,128)(2,1)}, bf16[2,768,128]{2,1,0:T(8,128)(2,1)S(1)}, u32[]{:S(2)}, u32[]{:S(2)}) collective-permute-start(bf16[2,768,128]{2,1,0:T(8,128)(2,1)} %dress.1.d2), channel_id=1, source_target_pairs={{32,0},{48,16},{64,32},{80,48},{96,64},{112,80},{128,96},{144,112}... | collective-permute-start | bytes 1179656 | tf_op jit(solution)/shard_map/ppermute | solution.py:18
  77.9 25.5 %collective-permute-start.2 = (bf16[2,768,128]{2,1,0:T(8,128)(2,1)}, bf16[2,768,128]{2,1,0:T(8,128)(2,1)S(1)}, u32[]{:S(2)}, u32[]{:S(2)}) collective-permute-start(bf16[2,768,128]{2,1,0:T(8,128)(2,1)} %dress.1.d2), channel_id=1, source_target_pairs={{16,0},{32,16},{48,32},{64,48},{80,64},{96,80},{112,96},{128,112},... | collective-permute-start | bytes 1179656 | tf_op jit(solution)/shard_map/ppermute | solution.py:18
  81.2 24.6 %collective-permute-start.1 = (bf16[2,768,128]{2,1,0:T(8,128)(2,1)}, bf16[2,768,128]{2,1,0:T(8,128)(2,1)S(1)}, u32[]{:S(2)}, u32[]{:S(2)}) collective-permute-start(bf16[2,768,128]{2,1,0:T(8,128)(2,1)} %dress.1.d2), channel_id=1, source_target_pairs={{0,16},{16,32},{32,48},{48,64},{64,80},{80,96},{96,112},{112,128},... | collective-permute-start | bytes 1179656 | tf_op jit(solution)/shard_map/ppermute | solution.py:18
  83.8 27.4 %collective-permute-start = (bf16[2,768,128]{2,1,0:T(8,128)(2,1)}, bf16[2,768,128]{2,1,0:T(8,128)(2,1)S(1)}, u32[]{:S(2)}, u32[]{:S(2)}) collective-permute-start(bf16[2,768,128]{2,1,0:T(8,128)(2,1)} %dress.1.d2), channel_id=1, source_target_pairs={{0,32},{16,48},{32,64},{48,80},{64,96},{80,112},{96,128},{112,144}... | collective-permute-start | bytes 1179656 | tf_op jit(solution)/shard_map/ppermute | solution.py:18
  94.9 16.3 %copy-start.2 = (bf16[2,768,128]{2,1,0:T(8,128)(2,1)}, bf16[2,768,128]{2,1,0:T(8,128)(2,1)S(1)}, u32[]{:S(2)}) copy-start(bf16[2,768,128]{2,1,0:T(8,128)(2,1)S(1)} %collective-permute-done.3.d4) | copy-start | bytes 1179652
  103.4 7.8 %copy-start.3 = (bf16[2,768,128]{2,1,0:T(8,128)(2,1)}, bf16[2,768,128]{2,1,0:T(8,128)(2,1)S(1)}, u32[]{:S(2)}) copy-start(bf16[2,768,128]{2,1,0:T(8,128)(2,1)S(1)} %collective-permute-done.2.d3) | copy-start | bytes 1179652
  105.8 5.4 %copy-start.4 = (bf16[2,768,128]{2,1,0:T(8,128)(2,1)}, bf16[2,768,128]{2,1,0:T(8,128)(2,1)S(1)}, u32[]{:S(2)}) copy-start(bf16[2,768,128]{2,1,0:T(8,128)(2,1)S(1)} %collective-permute-done.1.d1) | copy-start | bytes 1179652
  111.2 0.7 copy-start.5
where the time goes:
time: 128 us; the launch traced here: 127 us
  waiting for transfers between devices  72.5 us (57%)
  starting transfers between devices  25 us (20%)
  Pallas kernels  19.4 us (15%)
  local copies, waits for them, and re-layouts  7.27 us (6%)
  between operations  1.38 us (1%)
    all_to_all x1, waiting for transfers between devices, per_device(): lax.all_to_all(perambulator, 'col', split_axis=1, concat_axis=1, tiled=True)  49.7 us
    ppermute x4, waiting for transfers between devices, shifted(): return lax.ppermute(shard, axis, pairs)  22.8 us
    pallas_call x1, Pallas kernels, per_device(): pl.pallas_call(diagrams_kernel, out_shape=jax.ShapeDtypeStruct((slots, 2,...  14.8 us
    ppermute x4, starting transfers between devices, shifted(): return lax.ppermute(shard, axis, pairs)  14.5 us
    all_to_all x1, starting transfers between devices, per_device(): lax.all_to_all(perambulator, 'col', split_axis=1, concat_axis=1, tiled=True)  10.6 us
    pallas_call x1, Pallas kernels, per_device(): pl.pallas_call(dress_kernel, out_shape=jax.ShapeDtypeStruct((2, ndim, wid...  4.57 us
    unnamed x17, local copies, waits for them, and re-layouts  3.66 us
  transfers between devices with their start and end apart: 5, of which 5 were waited for; matrix products, arithmetic and copies ran while one was open for 5% of the time, Pallas kernels for 0%

commit v1 on v0

v1 whole, which is shorter than its diff:
```python
import jax
import jax.numpy as jnp
from jax import lax
from jax.experimental import pallas as pl
from jax.experimental.pallas import tpu as pltpu
from jax.sharding import PartitionSpec as P

DT = 2
TILE = 16
BF = jnp.bfloat16
F32 = jnp.float32


def shifted(shard, axis, by):
    count = lax.axis_size(axis)
    pairs = [(i, i + by) for i in range(count) if 0 <= i + by < count]
    return lax.ppermute(shard, axis, pairs)


def dot(left, right):
    return jnp.dot(left, right, preferred_element_type=F32)


def tau_copies(pieces, tau, sem):
    chunks, parts, depth, _ = pieces.shape
    return [
        pltpu.make_async_copy(
            pieces.at[c, part], tau.at[pl.ds((part * chunks + c) * depth, depth)], sem.at[part * chunks + c]
        )
        for part in range(parts)
        for c in range(chunks)
    ]


def spin_mix(split, gamma, adjoint, write, starts):
    for start in starts:
        part = [[split[c, pl.ds(4 * start + s, TILE, stride=4), :] for s in range(4)] for c in range(2)]
        for s in range(4):
            real = imag = None
            for q in range(4):
                if adjoint:
                    g_r, g_i = gamma[0, q, s], -gamma[1, q, s]
                else:
                    g_r, g_i = gamma[0, s, q], gamma[1, s, q]
                term_r = g_r * part[0][q] - g_i * part[1][q]
                term_i = g_r * part[1][q] + g_i * part[0][q]
                real = term_r if real is None else real + term_r
                imag = term_i if imag is None else imag + term_i
            write(start, s, real, imag)


def eigen_product(matrix, mixed, split, width):
    nev = matrix.shape[0]
    for c in range(2):
        for half in range(2):
            at = (2 * c + half) * 2 * width
            done = dot(matrix[...], mixed[:, at : at + 2 * width])
            for q in range(2):
                split[c, pl.ds(2 * half + q, nev, stride=4), :] = done[:, q * width : (q + 1) * width]


def dress_kernel(ident, gamma, pieces, sink_rows, forward, out, tau, split, mixed, sem):
    ndim, width = out.shape[1:]
    nev = ndim // 4
    copies = tau_copies(pieces, tau, sem)
    for copy in copies:
        copy.start()
    for copy in copies:
        copy.wait()
    for c in range(2):
        prop = dot(sink_rows[c * width : (c + 1) * width, :], tau[...])
        split[c] = prop.astype(BF).astype(F32).T

    def write(start, s, real, imag):
        rows = slice(start, start + TILE)
        low = slice(nev + start, nev + start + TILE)
        at_r = slice(s * width, (s + 1) * width)
        at_i = slice((4 + s) * width, (5 + s) * width)
        mixed[rows, at_r] = real.astype(BF)
        mixed[rows, at_i] = imag.astype(BF)
        mixed[low, at_r] = (-imag).astype(BF)
        mixed[low, at_i] = real.astype(BF)

    spin_mix(split, gamma, False, write, range(0, nev, TILE))
    eigen_product(forward.at[ident[0]], mixed, split, width)
    out[...] = split[...].astype(BF)


def diagrams_kernel(
    lists, count, position, gamma, pieces, d0, d1, d2, d3, d4, backward, out,
    tau, wide, mixed, rows, split, column, local, sem, block_sem,
):
    ndim, width = d0.shape[1:]
    nev = ndim // 4
    copies = tau_copies(pieces, tau, sem)
    blocks = [
        pltpu.make_async_copy(block, local.at[d], block_sem.at[d]) for d, block in enumerate((d0, d1, d2, d3, d4))
    ]
    for copy in blocks + copies:
        copy.start()
    for copy in blocks + copies:
        copy.wait()
    for d in range(2 * DT + 1):
        left = local[d, 0].T
        right = local[d, 1].T
        rows[d, :width, :ndim] = left
        rows[d, :width, ndim:] = -right
        rows[d, width:, :ndim] = right
        rows[d, width:, ndim:] = left
        split[d] = local[d].astype(F32)

        def write(start, s, real, imag):
            top = slice(start, start + TILE)
            low = slice(nev + start, nev + start + TILE)
            at_r = slice(s * width, (s + 1) * width)
            at_i = slice((4 + s) * width, (5 + s) * width)
            mixed[d, top, at_r] = real.astype(BF)
            mixed[d, top, at_i] = imag.astype(BF)
            mixed[d, low, at_r] = imag.astype(BF)
            mixed[d, low, at_i] = (-real).astype(BF)

        steps = range(0, ndim, 2 * width)
        share = nev // len(steps)
        for turn, at in enumerate(steps):
            product = dot(rows[d], tau[:, at : at + 2 * width]).astype(BF)
            wide[d, :, at : at + 2 * width] = product[:width]
            wide[d, :, ndim + at : ndim + at + 2 * width] = product[width:]
            spin_mix(split.at[d], gamma, True, write, range(turn * share, (turn + 1) * share, TILE))
    scale = (2.0 * ndim) ** (-0.5)
    offset = DT - position[0]
    for k in range(out.shape[0]):
        first = lists[k, 0] + offset
        second = lists[k, 1] + offset
        spread = split.at[k % split.shape[0]]
        eigen_product(backward.at[lists[k, 2]], mixed.at[first], spread, width)
        u_r = spread[0].astype(BF)
        u_i = spread[1].astype(BF)
        pair = column.at[k % 2]
        pair[:ndim, :width] = u_r
        pair[:ndim, width:] = u_i
        pair[ndim:, :width] = u_i
        pair[ndim:, width:] = -u_r
        result = dot(wide[second], pair[...]) * scale
        result = jnp.where(k < count[0], result, 0.0)
        out[k, 0] = result[:, :width]
        out[k, 1] = result[:, width:]


def per_device(
    perambulator, elementals, sink_block, gamma_spin, graph_lists, diagram_counts, source_ids
):
    ndim, width = sink_block.shape[1:]
    slots = graph_lists.shape[1]
    nev = elementals.shape[3]
    row_block = lax.all_to_all(perambulator, "col", split_axis=1, concat_axis=1, tiled=True)
    pieces = row_block[0]
    chunks = 2 * pieces.shape[0]
    table = elementals[0]
    sink_t = jnp.swapaxes(sink_block, 1, 2)
    sink_rows = jnp.concatenate(
        [
            jnp.concatenate([sink_t[0], -sink_t[1]], axis=1),
            jnp.concatenate([sink_t[1], sink_t[0]], axis=1),
        ],
        axis=0,
    )
    forward = jnp.concatenate([table[:, 0], table[:, 1]], axis=2)
    backward = jnp.concatenate(
        [jnp.swapaxes(table[:, 0], 1, 2), jnp.swapaxes(table[:, 1], 1, 2)], axis=2
    )
    smem = pl.BlockSpec(memory_space=pltpu.SMEM)
    vmem = pl.BlockSpec(memory_space=pltpu.VMEM)
    free = pl.BlockSpec(memory_space=pl.ANY)
    dressed = pl.pallas_call(
        dress_kernel,
        out_shape=jax.ShapeDtypeStruct((2, ndim, width), BF),
        in_specs=[smem, smem, free, vmem, vmem],
        out_specs=vmem,
        scratch_shapes=[
            pltpu.VMEM((2 * ndim, ndim), BF),
            pltpu.VMEM((2, ndim, width), F32),
            pltpu.VMEM((2 * nev, 8 * width), BF),
            pltpu.SemaphoreType.DMA((chunks,)),
        ],
        compiler_params=pltpu.CompilerParams(vmem_limit_bytes=16 << 20),
        name="dress",
    )(source_ids, gamma_spin, pieces, sink_rows, forward)
    up = shifted(dressed, "src", 1)
    down = shifted(dressed, "src", -1)
    up, down = lax.optimization_barrier((up, down))
    up_two = shifted(up, "src", 1)
    down_two = shifted(down, "src", -1)
    position = lax.axis_index("src").astype(jnp.int32).reshape(1)
    reach = 2 * DT + 1
    totals = pl.pallas_call(
        diagrams_kernel,
        out_shape=jax.ShapeDtypeStruct((slots, 2, width, width), F32),
        in_specs=[smem] * 4 + [free] * 6 + [vmem],
        out_specs=vmem,
        scratch_shapes=[
            pltpu.VMEM((2 * ndim, ndim), BF),
            pltpu.VMEM((reach, width, 2 * ndim), BF),
            pltpu.VMEM((reach, 2 * nev, 8 * width), BF),
            pltpu.VMEM((reach, 2 * width, 2 * ndim), BF),
            pltpu.VMEM((reach, 2, ndim, width), F32),
            pltpu.VMEM((2, 2 * ndim, 2 * width), BF),
            pltpu.VMEM((reach, 2, ndim, width), BF),
            pltpu.SemaphoreType.DMA((chunks,)),
            pltpu.SemaphoreType.DMA((reach,)),
        ],
        compiler_params=pltpu.CompilerParams(vmem_limit_bytes=32 << 20),
        name="diagrams",
    )(
        graph_lists[0], diagram_counts, position, gamma_spin, pieces,
        up_two, up, dressed, down, down_two, backward,
    )
    return totals[None, None]


def solution(mesh):
    in_specs = (
        P("src", None, None, "col", None),
        P("col", None, None, None, None),
        P(),
        P(),
        P("src", None, None),
        P("src"),
        P("src"),
    )
    out_specs = P("src", "col", None, None, None, None)
    return jax.shard_map(
        per_device, mesh=mesh, in_specs=in_specs, out_specs=out_specs, check_vma=False
    )
```

time: 128 us -> 123 us (0.961)
  waiting for transfers between devices: 72.5 us -> 67.5 us
  local copies, waits for them, and re-layouts: 7.27 us -> 5 us
    ppermute x4, waiting for transfers between devices: 22.8 us -> 17.2 us  [shifted(): return lax.ppermute(shard, axis, pairs)]
    unnamed x17 -> x10, local copies, waits for them, and re-layouts: 3.66 us -> 2.73 us
  transfers between devices with their start and end apart: 5 -> 5, of which waited for: 5 -> 5; matrix products, arithmetic and copies ran while one was open for 5% -> 4% of each run, Pallas kernels for 0% -> 0%
where the time goes in v1:
time: 123 us; the launch traced here: 122 us
  waiting for transfers between devices  67.5 us (55%)
  starting transfers between devices  26.2 us (21%)
  Pallas kernels  20 us (16%)
  local copies, waits for them, and re-layouts  5 us (4%)
  between operations  1.56 us (1%)
  other arithmetic  1.53 us (1%)
    all_to_all x1, waiting for transfers between devices, per_device(): lax.all_to_all(perambulator, 'col', split_axis=1, concat_axis=1, tiled=True)  50.2 us
    ppermute x4, waiting for transfers between devices, shifted(): return lax.ppermute(shard, axis, pairs)  17.2 us
    ppermute x4, starting transfers between devices, shifted(): return lax.ppermute(shard, axis, pairs)  15.7 us
    pallas_call x1, Pallas kernels, per_device(): pl.pallas_call(diagrams_kernel, out_shape=jax.ShapeDtypeStruct((slots, 2,...  14.4 us
    all_to_all x1, starting transfers between devices, per_device(): lax.all_to_all(perambulator, 'col', split_axis=1, concat_axis=1, tiled=True)  10.6 us
    pallas_call x1, Pallas kernels, per_device(): pl.pallas_call(dress_kernel, out_shape=jax.ShapeDtypeStruct((2, ndim, wid...  5.65 us
    unnamed x10, local copies, waits for them, and re-layouts  2.73 us
  transfers between devices with their start and end apart: 5, of which 5 were waited for; matrix products, arithmetic and copies ran while one was open for 4% of the time, Pallas kernels for 0%

profile of v1, /device:TPU:6, one launch (start us, length us, event | category | flops | bytes accessed | tf_op | source)
XLA Modules:
  0.0 121.8 jit_solution(5919833510515503342)
XLA Ops:
  0.0 0.0 copy-start.2
  0.0 10.6 %all-to-all-start = ((bf16[1,16,2,48,768]{4,3,2,0,1:T(8,128)(2,1)}), bf16[1,16,2,48,768]{4,3,2,0,1:T(8,128)(2,1)S(1)}, u32[]{:S(2)}, u32[]{:S(2)}) async-start(bf16[1,16,2,48,768]{4,3,2,0,1:T(8,128)(2,1)} %bitcast.29), calls=%async_computation | async-start | bytes 4718592 | tf_op jit(solution)/shard_map/all_to_all | solution.py:155
  11.2 0.0 copy-done.2
  11.2 0.2 copy.13
  11.4 1.5 %copy.14 = bf16[1,4,2,192,192]{3,4,1,2,0:T(8,128)(2,1)S(1)} copy(bf16[1,4,2,192,192]{4,3,2,1,0:T(8,128)(2,1)} %param.8) | data formatting | bytes 1179648 | tf_op args[1]
  12.9 1.1 slice_bitcast_fusion.2
  13.9 0.1 pad_maximum_fusion
  14.1 1.1 copy.15.forward
  15.2 0.0 copy-start.1
  15.2 0.1 maximum_maximum_fusion.sink_rows
  15.3 50.2 %all-to-all-done = bf16[1,16,2,48,768]{4,3,2,0,1:T(8,128)(2,1)S(1)} async-done(((bf16[1,16,2,48,768]{4,3,2,0,1:T(8,128)(2,1)}), bf16[1,16,2,48,768]{4,3,2,0,1:T(8,128)(2,1)S(1)}, u32[]{:S(2)}, u32[]{:S(2)}) %all-to-all-start) | async-done | bytes 2359328 | tf_op jit(solution)/shard_map/all_to_all | solution.py:155
  65.5 0.0 copy-done.1
  65.5 0.0 copy-start
  65.5 1.1 copy-done
  66.6 0.0 copy-start.3
  66.6 5.7 %dress.1.d2 = bf16[2,768,128]{2,1,0:T(8,128)(2,1)S(1)} custom-call(s32[1]{0:T(128)S(6)} %copy.19.ident, f32[2,4,4]{2,1,0:T(4,128)S(1)} %copy-done.1, bf16[16,2,48,768]{3,2,1,0:T(8,128)(2,1)S(1)} %bitcast.23, bf16[256,1536]{1,0:T(8,128)(2,1)S(1)} %maximum_maximum_fusion.sink_rows, bf16[4,192,384]{2,1,0:T(8,128)(2,1)S(1)} %copy-done), custom_call_target="tpu_custom_call" | custom-call | tf_op jit(solution)/shard_map/dress/pallas_call | solution.py:174
  72.2 5.6 %collective-permute-start.1 = (bf16[2,768,128]{2,1,0:T(8,128)(2,1)S(1)}, bf16[2,768,128]{2,1,0:T(8,128)(2,1)S(1)}, u32[]{:S(2)}, u32[]{:S(2)}) collective-permute-start(bf16[2,768,128]{2,1,0:T(8,128)(2,1)S(1)} %dress.1.d2), channel_id=1, source_target_pairs={{16,0},{32,16},{48,32},{64,48},{80,64},{96,80},{112,96},{128,112},... | collective-permute-start | bytes 1179656 | tf_op jit(solution)/shard_map/ppermute | solution.py:17
  77.9 1.9 %collective-permute-start = (bf16[2,768,128]{2,1,0:T(8,128)(2,1)S(1)}, bf16[2,768,128]{2,1,0:T(8,128)(2,1)S(1)}, u32[]{:S(2)}, u32[]{:S(2)}) collective-permute-start(bf16[2,768,128]{2,1,0:T(8,128)(2,1)S(1)} %dress.1.d2), channel_id=1, source_target_pairs={{0,16},{16,32},{32,48},{48,64},{64,80},{80,96},{96,112},{112,128},... | collective-permute-start | bytes 1179656 | tf_op jit(solution)/shard_map/ppermute | solution.py:17
  79.8 6.4 %collective-permute-done.1.d3 = bf16[2,768,128]{2,1,0:T(8,128)(2,1)S(1)} collective-permute-done((bf16[2,768,128]{2,1,0:T(8,128)(2,1)S(1)}, bf16[2,768,128]{2,1,0:T(8,128)(2,1)S(1)}, u32[]{:S(2)}, u32[]{:S(2)}) %collective-permute-start.1) | collective-permute-done | bytes 393248 | tf_op jit(solution)/shard_map/ppermute | solution.py:17
  86.2 6.2 %collective-permute-done.d1 = bf16[2,768,128]{2,1,0:T(8,128)(2,1)S(1)} collective-permute-done((bf16[2,768,128]{2,1,0:T(8,128)(2,1)S(1)}, bf16[2,768,128]{2,1,0:T(8,128)(2,1)S(1)}, u32[]{:S(2)}, u32[]{:S(2)}) %collective-permute-start) | collective-permute-done | bytes 393248 | tf_op jit(solution)/shard_map/ppermute | solution.py:17
  92.4 1.9 %collective-permute-start.2 = (bf16[2,768,128]{2,1,0:T(8,128)(2,1)S(1)}, bf16[2,768,128]{2,1,0:T(8,128)(2,1)}, u32[]{:S(2)}, u32[]{:S(2)}) collective-permute-start(bf16[2,768,128]{2,1,0:T(8,128)(2,1)S(1)} %collective-permute-done.d1), channel_id=1, source_target_pairs={{0,16},{16,32},{32,48},{48,64},{64,80},{80,96},{96,112},{112,128},... | collective-permute-start | bytes 1179656 | tf_op jit(solution)/shard_map/ppermute | solution.py:17
  94.3 6.2 %collective-permute-start.3 = (bf16[2,768,128]{2,1,0:T(8,128)(2,1)S(1)}, bf16[2,768,128]{2,1,0:T(8,128)(2,1)}, u32[]{:S(2)}, u32[]{:S(2)}) collective-permute-start(bf16[2,768,128]{2,1,0:T(8,128)(2,1)S(1)} %collective-permute-done.1.d3), channel_id=1, source_target_pairs={{16,0},{32,16},{48,32},{64,48},{80,64},{96,80},{112,96},{128,112},... | collective-permute-start | bytes 1179656 | tf_op jit(solution)/shard_map/ppermute | solution.py:17
  101.2 0.0 copy-done.3
  101.2 0.1 copy.17
  101.3 1.3 %pad_maximum_fusion.1.backward = bf16[4,192,384]{2,1,0:T(8,128)(2,1)S(1)} fusion(bf16[4,192,192]{2,1,0:T(8,128)(2,1)} %get-tuple-element.10, bf16[4,192,192]{2,1,0:T(8,128)(2,1)} %get-tuple-element.9), kind=kLoop, calls=%fused_computation.2 | loop fusion | flops 1179648 | bytes 1179648 | tf_op jit(solution)/shard_map/concatenate | solution.py:168
  102.6 3.5 %collective-permute-done.2.d0 = bf16[2,768,128]{2,1,0:T(8,128)(2,1)} collective-permute-done((bf16[2,768,128]{2,1,0:T(8,128)(2,1)S(1)}, bf16[2,768,128]{2,1,0:T(8,128)(2,1)}, u32[]{:S(2)}, u32[]{:S(2)}) %collective-permute-start.2) | collective-permute-done | bytes 393248 | tf_op jit(solution)/shard_map/ppermute | solution.py:17
  106.2 1.1 collective-permute-done.3.d4
  107.3 14.4 %diagrams.1 = f32[6,2,128,128]{3,2,1,0:T(8,128)} custom-call(s32[6,3]{1,0:T(8,128)S(1)} %bitcast.25, s32[1]{0:T(128)S(6)} %copy.18.count, s32[1]{0:T(128)} %bitcast.1.position, f32[2,4,4]{2,1,0:T(4,128)S(1)} %copy-done.1, bf16[16,2,48,768]{3,2,1,0:T(8,128)(2,1)S(1)} %bitcast.24, bf16[2,768,128]{2,1,0:T(8,128)(2,1)} %collective-permute-done.2.d0, ...), custom_call_target="tpu_custom_call" | custom-call | tf_op jit(solution)/shard_map/diagrams/pallas_call | solution.py:195
  (2 shorter events, 0.0 us)
Async XLA Ops:
  0.0 11.2 %copy-start.2 = (bf16[2,768,128]{2,1,0:T(8,128)(2,1)S(1)}, bf16[2,768,128]{2,1,0:T(8,128)(2,1)}, u32[]{:S(2)}) copy-start(bf16[2,768,128]{2,1,0:T(8,128)(2,1)} %param.9) | copy-start | bytes 1179652
  0.0 65.5 %all-to-all-start = ((bf16[1,16,2,48,768]{4,3,2,0,1:T(8,128)(2,1)}), bf16[1,16,2,48,768]{4,3,2,0,1:T(8,128)(2,1)S(1)}, u32[]{:S(2)}, u32[]{:S(2)}) async-start(bf16[1,16,2,48,768]{4,3,2,0,1:T(8,128)(2,1)} %bitcast.29), calls=%async_computation | async-start | bytes 4718592 | tf_op jit(solution)/shard_map/all_to_all | solution.py:155
  15.2 50.4 %copy-start.1 = (f32[2,4,4]{2,1,0:T(4,128)S(1)}, f32[2,4,4]{2,1,0:T(4,128)}, u32[]{:S(2)}) copy-start(f32[2,4,4]{2,1,0:T(4,128)} %gamma.3) | copy-start | bytes 388
  65.5 1.1 copy-start
  66.6 34.6 %copy-start.3 = (s32[1,6,3]{1,0,2:T(1,128)S(1)}, s32[1,6,3]{1,0,2:T(1,128)}, u32[]{:S(2)}) copy-start(s32[1,6,3]{1,0,2:T(1,128)} %param.11) | copy-start | bytes 220
  72.2 13.9 %collective-permute-start.1 = (bf16[2,768,128]{2,1,0:T(8,128)(2,1)S(1)}, bf16[2,768,128]{2,1,0:T(8,128)(2,1)S(1)}, u32[]{:S(2)}, u32[]{:S(2)}) collective-permute-start(bf16[2,768,128]{2,1,0:T(8,128)(2,1)S(1)} %dress.1.d2), channel_id=1, source_target_pairs={{16,0},{32,16},{48,32},{64,48},{80,64},{96,80},{112,96},{128,112},... | collective-permute-start | bytes 1179656 | tf_op jit(solution)/shard_map/ppermute | solution.py:17
  77.9 14.5 %collective-permute-start = (bf16[2,768,128]{2,1,0:T(8,128)(2,1)S(1)}, bf16[2,768,128]{2,1,0:T(8,128)(2,1)S(1)}, u32[]{:S(2)}, u32[]{:S(2)}) collective-permute-start(bf16[2,768,128]{2,1,0:T(8,128)(2,1)S(1)} %dress.1.d2), channel_id=1, source_target_pairs={{0,16},{16,32},{32,48},{48,64},{64,80},{80,96},{96,112},{112,128},... | collective-permute-start | bytes 1179656 | tf_op jit(solution)/shard_map/ppermute | solution.py:17
  92.4 13.8 %collective-permute-start.2 = (bf16[2,768,128]{2,1,0:T(8,128)(2,1)S(1)}, bf16[2,768,128]{2,1,0:T(8,128)(2,1)}, u32[]{:S(2)}, u32[]{:S(2)}) collective-permute-start(bf16[2,768,128]{2,1,0:T(8,128)(2,1)S(1)} %collective-permute-done.d1), channel_id=1, source_target_pairs={{0,16},{16,32},{32,48},{48,64},{64,80},{80,96},{96,112},{112,128},... | collective-permute-start | bytes 1179656 | tf_op jit(solution)/shard_map/ppermute | solution.py:17
  94.3 12.9 %collective-permute-start.3 = (bf16[2,768,128]{2,1,0:T(8,128)(2,1)S(1)}, bf16[2,768,128]{2,1,0:T(8,128)(2,1)}, u32[]{:S(2)}, u32[]{:S(2)}) collective-permute-start(bf16[2,768,128]{2,1,0:T(8,128)(2,1)S(1)} %collective-permute-done.1.d3), channel_id=1, source_target_pairs={{16,0},{32,16},{48,32},{64,48},{80,64},{96,80},{112,96},{128,112},... | collective-permute-start | bytes 1179656 | tf_op jit(solution)/shard_map/ppermute | solution.py:17

commit v2 on v1

v2 whole, which is shorter than its diff:
```python
import functools

import jax
import jax.numpy as jnp
from jax import lax
from jax.experimental import pallas as pl
from jax.experimental.pallas import tpu as pltpu
from jax.sharding import PartitionSpec as P

DT = 2
TILE = 16
BF = jnp.bfloat16
F32 = jnp.float32


def swapped(shard, axis, start):
    count = lax.axis_size(axis)
    lower = range(start, count - 1, 2)
    return lax.ppermute(shard, axis, [(i, i + 1) for i in lower] + [(i + 1, i) for i in lower])


def dot(left, right):
    return jnp.dot(left, right, preferred_element_type=F32)


def stack_rows(real, imag, target, depth):
    width = real.shape[1]
    for at in range(0, real.shape[0], depth):
        upper = slice(2 * at, 2 * at + depth)
        lower = slice(2 * at + depth, 2 * at + 2 * depth)
        target[upper, :width] = real[at : at + depth]
        target[upper, width:] = imag[at : at + depth]
        target[lower, :width] = -imag[at : at + depth]
        target[lower, width:] = real[at : at + depth]


def spin_mix(split, gamma, adjoint, write, starts):
    for start in starts:
        part = [[split[c, pl.ds(4 * start + s, TILE, stride=4), :] for s in range(4)] for c in range(2)]
        for s in range(4):
            real = imag = None
            for q in range(4):
                if adjoint:
                    g_r, g_i = gamma[0, q, s], -gamma[1, q, s]
                else:
                    g_r, g_i = gamma[0, s, q], gamma[1, s, q]
                term_r = g_r * part[0][q] - g_i * part[1][q]
                term_i = g_r * part[1][q] + g_i * part[0][q]
                real = term_r if real is None else real + term_r
                imag = term_i if imag is None else imag + term_i
            write(start, s, real, imag)


def eigen_product(product, nev, split, width):
    for c in range(2):
        for half in range(2):
            at = (2 * c + half) * 2 * width
            done = product(slice(at, at + 2 * width))
            for q in range(2):
                split[c, pl.ds(2 * half + q, nev, stride=4), :] = done[:, q * width : (q + 1) * width]


def dress_kernel(ident, gamma, tau, sink, forward, out, split, mixed, matrix, rows, sem, *, depth):
    ndim, width = out.shape[1:]
    nev = ndim // 4
    fetch = pltpu.make_async_copy(forward.at[ident[0]], matrix, sem)
    fetch.start()
    stack_rows(sink[0], sink[1], rows, depth)
    left = rows[...].T
    for at in range(0, ndim, 2 * width):
        prop = dot(left, tau[:, at : at + 2 * width]).astype(BF).astype(F32)
        split[0, at : at + 2 * width, :] = prop[:width].T
        split[1, at : at + 2 * width, :] = prop[width:].T

    def write(start, s, real, imag):
        rows = slice(start, start + TILE)
        low = slice(nev + start, nev + start + TILE)
        at_r = slice(s * width, (s + 1) * width)
        at_i = slice((4 + s) * width, (5 + s) * width)
        mixed[rows, at_r] = real.astype(BF)
        mixed[rows, at_i] = imag.astype(BF)
        mixed[low, at_r] = (-imag).astype(BF)
        mixed[low, at_i] = real.astype(BF)

    spin_mix(split, gamma, False, write, range(0, nev, TILE))
    fetch.wait()

    def product(at):
        return dot(matrix[0], mixed[:nev, at]) + dot(matrix[1], mixed[nev:, at])

    eigen_product(product, nev, split, width)
    out[...] = split[...].astype(BF)


def prepare(d, block, gamma, tau, wide, mixed, rows, split, depth):
    ndim, width = block.shape[1:]
    nev = ndim // 4
    split[...] = block[...].astype(F32)

    def write(start, s, real, imag):
        top = slice(start, start + TILE)
        low = slice(nev + start, nev + start + TILE)
        at_r = slice(s * width, (s + 1) * width)
        at_i = slice((4 + s) * width, (5 + s) * width)
        mixed[d, top, at_r] = real.astype(BF)
        mixed[d, top, at_i] = imag.astype(BF)
        mixed[d, low, at_r] = imag.astype(BF)
        mixed[d, low, at_i] = (-real).astype(BF)

    spin_mix(split, gamma, True, write, range(0, nev, TILE))
    stack_rows(block[0], block[1], rows, depth)
    left = rows[...].T
    for at in range(0, ndim, 2 * width):
        product = dot(left, tau[:, at : at + 2 * width]).astype(BF)
        wide[d, :, at : at + 2 * width] = product[:width]
        wide[d, :, ndim + at : ndim + at + 2 * width] = product[width:]


def prepare_kernel(*refs, depth, entries, fresh):
    gamma, tau = refs[:2]
    blocks = refs[2 : 2 + len(entries)]
    rest = refs[2 + len(entries) + (0 if fresh else 2) :]
    wide, mixed, rows, split = rest
    for turn, (d, block) in enumerate(zip(entries, blocks)):
        prepare(d, block, gamma, tau, wide, mixed, rows.at[turn], split.at[turn], depth)


def diagrams_kernel(
    lists, count, position, gamma, tau, low, high, backward, wide_in, mixed_in, out, wide, mixed,
    rows, split, column, *, depth,
):
    ndim, width = low.shape[1:]
    nev = ndim // 4
    prepare(3, low, gamma, tau, wide, mixed, rows.at[0], split.at[0], depth)
    prepare(4, high, gamma, tau, wide, mixed, rows.at[1], split.at[1], depth)
    scale = (2.0 * ndim) ** (-0.5)
    here = position[0]
    sign = 1 - 2 * (here % 2)

    def entry(sender):
        ahead = (sender - here) * sign
        near = jnp.where(ahead == 1, 1, 2)
        far = jnp.where(ahead == 2, 3, 4)
        return jnp.where(ahead == 0, 0, jnp.where(ahead * ahead == 1, near, far))

    for k in range(out.shape[0]):
        first = entry(lists[k, 0])
        second = entry(lists[k, 1])
        spread = split.at[k % 2]

        def product(at):
            return dot(backward[lists[k, 2]], mixed[first, :, at])

        eigen_product(product, nev, spread, width)
        u_r = spread[0].astype(BF)
        u_i = spread[1].astype(BF)
        pair = column.at[k % 2]
        pair[:ndim, :width] = u_r
        pair[:ndim, width:] = u_i
        pair[ndim:, :width] = u_i
        pair[ndim:, width:] = -u_r
        result = dot(wide[second], pair[...]) * scale
        result = jnp.where(k < count[0], result, 0.0)
        out[k, 0] = result[:, :width]
        out[k, 1] = result[:, width:]


def per_device(
    perambulator, elementals, sink_block, gamma_spin, graph_lists, diagram_counts, source_ids
):
    ndim, width = sink_block.shape[1:]
    slots = graph_lists.shape[1]
    nev = elementals.shape[3]
    depth = perambulator.shape[3]
    reach = 2 * DT + 1
    row_block = lax.all_to_all(perambulator, "col", split_axis=1, concat_axis=1, tiled=True)
    tau = row_block.reshape(2 * ndim, ndim)
    table = elementals[0]
    backward = jnp.concatenate(
        [jnp.swapaxes(table[:, 0], 1, 2), jnp.swapaxes(table[:, 1], 1, 2)], axis=2
    )
    tau, backward = lax.optimization_barrier((tau, backward))
    smem = pl.BlockSpec(memory_space=pltpu.SMEM)
    vmem = pl.BlockSpec(memory_space=pltpu.VMEM)
    free = pl.BlockSpec(memory_space=pl.ANY)

    def scratch(count):
        return [
            pltpu.VMEM((count, 2 * ndim, 2 * width), BF),
            pltpu.VMEM((2, 2, ndim, width), F32),
        ]

    dressed = pl.pallas_call(
        functools.partial(dress_kernel, depth=depth),
        out_shape=jax.ShapeDtypeStruct((2, ndim, width), BF),
        in_specs=[smem, smem, vmem, vmem, free],
        out_specs=vmem,
        scratch_shapes=[
            pltpu.VMEM((2, ndim, width), F32),
            pltpu.VMEM((2 * nev, 8 * width), BF),
            pltpu.VMEM((2, nev, nev), BF),
            pltpu.VMEM((2 * ndim, 2 * width), BF),
            pltpu.SemaphoreType.DMA,
        ],
        compiler_params=pltpu.CompilerParams(vmem_limit_bytes=10 << 20),
        name="dress",
    )(source_ids, gamma_spin, tau, sink_block, table)
    state = (
        jax.ShapeDtypeStruct((reach, width, 2 * ndim), BF),
        jax.ShapeDtypeStruct((reach, 2 * nev, 8 * width), BF),
    )

    def prepared(blocks, entries, held=()):
        fresh = not held
        count = 2 + len(blocks)
        return pl.pallas_call(
            functools.partial(prepare_kernel, depth=depth, entries=entries, fresh=fresh),
            out_shape=state,
            in_specs=[smem, vmem] + [vmem] * (len(blocks) + len(held)),
            out_specs=(vmem, vmem),
            scratch_shapes=scratch(len(blocks)),
            input_output_aliases={} if fresh else {count: 0, count + 1: 1},
            compiler_params=pltpu.CompilerParams(vmem_limit_bytes=12 << 20),
            name="prepare",
        )(gamma_spin, tau, *blocks, *held)

    even = swapped(dressed, "src", 0)
    odd = swapped(dressed, "src", 1)
    held = prepared((dressed,), (0,))
    odd_far = swapped(even, "src", 1)
    even_far = swapped(odd, "src", 0)
    held = prepared((even, odd), (1, 2), held)
    position = lax.axis_index("src").astype(jnp.int32).reshape(1)
    totals, _, _ = pl.pallas_call(
        functools.partial(diagrams_kernel, depth=depth),
        out_shape=(jax.ShapeDtypeStruct((slots, 2, width, width), F32), *state),
        in_specs=[smem] * 4 + [vmem] * 6,
        out_specs=(vmem, vmem, vmem),
        scratch_shapes=scratch(2) + [pltpu.VMEM((2, 2 * ndim, 2 * width), BF)],
        input_output_aliases={8: 1, 9: 2},
        compiler_params=pltpu.CompilerParams(vmem_limit_bytes=16 << 20),
        name="diagrams",
    )(
        graph_lists[0], diagram_counts, position, gamma_spin, tau, even_far, odd_far, backward, *held
    )
    return totals[None, None]


def solution(mesh):
    in_specs = (
        P("src", None, None, "col", None),
        P("col", None, None, None, None),
        P(),
        P(),
        P("src", None, None),
        P("src"),
        P("src"),
    )
    out_specs = P("src", "col", None, None, None, None)
    return jax.shard_map(
        per_device, mesh=mesh, in_specs=in_specs, out_specs=out_specs, check_vma=False
    )
```

time: 123 us -> 108 us (0.88)
  waiting for transfers between devices: 67.5 us -> 58.4 us
  Pallas kernels: 20 us -> 15.8 us
  local copies, waits for them, and re-layouts: 5 us -> 3.5 us
    ppermute x4, waiting for transfers between devices: 17.2 us -> 7.56 us  [swapped(): lax.ppermute(shard, axis, [(i, i + 1) for i in lower] + [(i + 1, i) for i...]
    pallas_call x2 -> x4, Pallas kernels: 20 us -> 15.8 us  [the longest x1 7.3 us: per_device(): pl.pallas_call(functools.partial(diagrams_kernel, depth=depth), out_shape...]
    unnamed x10 -> x11, local copies, waits for them, and re-layouts: 2.73 us -> 2.24 us
  transfers between devices with their start and end apart: 5 -> 5, of which waited for: 5 -> 4; matrix products, arithmetic and copies ran while one was open for 4% -> 3% of each run, Pallas kernels for 0% -> 5%
where the time goes in v2:
time: 108 us; the launch traced here: 107 us
  waiting for transfers between devices  58.4 us (54%)
  starting transfers between devices  27 us (25%)
  Pallas kernels  15.8 us (15%)
  local copies, waits for them, and re-layouts  3.5 us (3%)
  between operations  1.41 us (1%)
    all_to_all x1, waiting for transfers between devices, per_device(): lax.all_to_all(perambulator, 'col', split_axis=1, concat_axis=1, tiled=True)  50.9 us
    ppermute x4, starting transfers between devices, swapped(): lax.ppermute(shard, axis, [(i, i + 1) for i in lower] + [(i + 1, i) for i...  16.4 us
    all_to_all x1, starting transfers between devices, per_device(): lax.all_to_all(perambulator, 'col', split_axis=1, concat_axis=1, tiled=True)  10.6 us
    ppermute x4, waiting for transfers between devices, swapped(): lax.ppermute(shard, axis, [(i, i + 1) for i in lower] + [(i + 1, i) for i...  7.56 us
    pallas_call x1, Pallas kernels, per_device(): pl.pallas_call(functools.partial(diagrams_kernel, depth=depth), out_shape...  7.3 us
    pallas_call x2, Pallas kernels, prepared(): pl.pallas_call(functools.partial(prepare_kernel, depth=depth, entries=ent...  5.48 us
    pallas_call x1, Pallas kernels, per_device(): pl.pallas_call(functools.partial(dress_kernel, depth=depth), out_shape=ja...  3.02 us
    unnamed x11, local copies, waits for them, and re-layouts  2.24 us
  transfers between devices with their start and end apart: 5, of which 4 were waited for; matrix products, arithmetic and copies ran while one was open for 3% of the time, Pallas kernels for 5%

profile of v2, /device:TPU:6, one launch (start us, length us, event | category | flops | bytes accessed | tf_op | source)
XLA Modules:
  0.0 107.2 jit_solution(11681135067577362437)
XLA Ops:
  0.0 0.0 copy-start
  0.0 10.6 %all-to-all-start = ((bf16[1,16,2,48,768]{4,3,2,0,1:T(8,128)(2,1)}), bf16[1,16,2,48,768]{4,3,2,0,1:T(8,128)(2,1)S(1)}, u32[]{:S(2)}, u32[]{:S(2)}) async-start(bf16[1,16,2,48,768]{4,3,2,0,1:T(8,128)(2,1)} %bitcast.22), calls=%async_computation | async-start | bytes 4718592 | tf_op jit(solution)/shard_map/all_to_all | solution.py:176
  11.2 0.0 copy-done
  11.2 0.0 copy-start.3
  11.2 1.2 %copy.16 = bf16[1,4,2,192,192]{3,4,1,2,0:T(8,128)(2,1)} copy(bf16[1,4,2,192,192]{4,3,2,1,0:T(8,128)(2,1)S(1)} %copy-done) | data formatting | bytes 1179648 | tf_op args[1]
  12.5 1.2 %slice_bitcast_fusion.1 = (bf16[4,192,192]{2,1,0:T(8,128)(2,1)S(1)}, bf16[4,192,192]{2,1,0:T(8,128)(2,1)S(1)}) fusion(bf16[4,2,192,192]{2,3,0,1:T(8,128)(2,1)} %bitcast.21), kind=kLoop, calls=%fused_computation.2 | loop fusion | bytes 1179648 | tf_op jit(solution)/shard_map/transpose | solution.py:180
  13.6 1.0 pad_maximum_fusion.backward
  14.7 50.9 %all-to-all-done = bf16[1,16,2,48,768]{4,3,2,0,1:T(8,128)(2,1)S(1)} async-done(((bf16[1,16,2,48,768]{4,3,2,0,1:T(8,128)(2,1)}), bf16[1,16,2,48,768]{4,3,2,0,1:T(8,128)(2,1)S(1)}, u32[]{:S(2)}, u32[]{:S(2)}) %all-to-all-start) | async-done | bytes 2359328 | tf_op jit(solution)/shard_map/all_to_all | solution.py:176
  65.5 0.0 copy-done.3
  65.5 0.0 copy-start.2
  65.5 1.0 copy-done.2
  66.5 0.0 copy-start.4
  66.5 3.0 %dress.1.refs_2_ = bf16[2,768,128]{2,1,0:T(8,128)(2,1)S(1)} custom-call(s32[1]{0:T(128)S(6)} %copy.26.ident, f32[2,4,4]{2,1,0:T(4,128)S(1)} %copy-done.3, bf16[1536,768]{1,0:T(8,128)(2,1)S(1)} %bitcast.15, bf16[2,768,128]{2,1,0:T(8,128)(2,1)S(1)} %copy-done.2, bf16[4,2,192,192]{3,2,1,0:T(8,128)(2,1)S(1)} %bitcast.19), custom_call_target="tpu_custom_call" | custom-call | tf_op jit(solution)/shard_map/dress/pallas_call | solution.py:193
  69.5 3.5 %collective-permute-start.2 = (bf16[2,768,128]{2,1,0:T(8,128)(2,1)S(1)}, bf16[2,768,128]{2,1,0:T(8,128)(2,1)S(1)}, u32[]{:S(2)}, u32[]{:S(2)}) collective-permute-start(bf16[2,768,128]{2,1,0:T(8,128)(2,1)S(1)} %dress.1.refs_2_), channel_id=1, source_target_pairs={{0,16},{32,48},{64,80},{96,112},{128,144},{160,176},{192,208},{224... | collective-permute-start | bytes 1179656 | tf_op jit(solution)/shard_map/ppermute | solution.py:19
  73.0 5.4 %collective-permute-start = (bf16[2,768,128]{2,1,0:T(8,128)(2,1)S(1)}, bf16[2,768,128]{2,1,0:T(8,128)(2,1)}, u32[]{:S(2)}, u32[]{:S(2)}) collective-permute-start(bf16[2,768,128]{2,1,0:T(8,128)(2,1)S(1)} %dress.1.refs_2_), channel_id=1, source_target_pairs={{16,32},{48,64},{80,96},{112,128},{144,160},{176,192},{208,224},{2... | collective-permute-start | bytes 1179656 | tf_op jit(solution)/shard_map/ppermute | solution.py:19
  78.5 3.8 %collective-permute-done.2.refs_2_ = bf16[2,768,128]{2,1,0:T(8,128)(2,1)S(1)} collective-permute-done((bf16[2,768,128]{2,1,0:T(8,128)(2,1)S(1)}, bf16[2,768,128]{2,1,0:T(8,128)(2,1)S(1)}, u32[]{:S(2)}, u32[]{:S(2)}) %collective-permute-start.2) | collective-permute-done | bytes 393248 | tf_op jit(solution)/shard_map/ppermute | solution.py:19
  82.2 5.6 %collective-permute-start.3 = (bf16[2,768,128]{2,1,0:T(8,128)(2,1)S(1)}, bf16[2,768,128]{2,1,0:T(8,128)(2,1)S(1)}, u32[]{:S(2)}, u32[]{:S(2)}) collective-permute-start(bf16[2,768,128]{2,1,0:T(8,128)(2,1)S(1)} %collective-permute-done.2.refs_2_), channel_id=1, source_target_pairs={{16,32},{48,64},{80,96},{112,128},{144,160},{176,192},{208,224},{2... | collective-permute-start | bytes 1179656 | tf_op jit(solution)/shard_map/ppermute | solution.py:19
  87.9 0.0 collective-permute-done.refs_3_
  87.9 1.9 %collective-permute-start.1 = (bf16[2,768,128]{2,1,0:T(8,128)(2,1)}, bf16[2,768,128]{2,1,0:T(8,128)(2,1)}, u32[]{:S(2)}, u32[]{:S(2)}) collective-permute-start(bf16[2,768,128]{2,1,0:T(8,128)(2,1)} %collective-permute-done.refs_3_), channel_id=1, source_target_pairs={{0,16},{32,48},{64,80},{96,112},{128,144},{160,176},{192,208},{224... | collective-permute-start | bytes 1179656 | tf_op jit(solution)/shard_map/ppermute | solution.py:19
  90.5 0.0 copy-done.4
  90.5 0.1 copy.19
  90.6 2.0 %prepare.2 = (bf16[5,128,1536]{2,1,0:T(8,128)(2,1)S(1)}, bf16[5,384,1024]{2,1,0:T(8,128)(2,1)S(1)}) custom-call(f32[2,4,4]{2,1,0:T(4,128)S(1)} %copy-done.3, bf16[1536,768]{1,0:T(8,128)(2,1)S(1)} %bitcast.16, bf16[2,768,128]{2,1,0:T(8,128)(2,1)S(1)} %dress.1.refs_2_), custom_call_target="tpu_custom_call" | custom-call | tf_op jit(solution)/shard_map/prepare/pallas_call | solution.py:216
  92.5 0.0 copy-start.1
  92.5 3.5 %prepare.3 = (bf16[5,128,1536]{2,1,0:T(8,128)(2,1)S(1)}, bf16[5,384,1024]{2,1,0:T(8,128)(2,1)S(1)}) custom-call(f32[2,4,4]{2,1,0:T(4,128)S(1)} %copy-done.3, bf16[1536,768]{1,0:T(8,128)(2,1)S(1)} %bitcast.17, bf16[2,768,128]{2,1,0:T(8,128)(2,1)S(1)} %collective-permute-done.2.refs_2_, ...), custom_call_target="tpu_custom_call", output_to_operand_aliasing={{0}: (4, {}), {1}: (5, {})} | custom-call | tf_op jit(solution)/shard_map/prepare/pallas_call | solution.py:216
  96.1 0.2 collective-permute-done.3.high
  96.3 3.6 %collective-permute-done.1.low = bf16[2,768,128]{2,1,0:T(8,128)(2,1)} collective-permute-done((bf16[2,768,128]{2,1,0:T(8,128)(2,1)}, bf16[2,768,128]{2,1,0:T(8,128)(2,1)}, u32[]{:S(2)}, u32[]{:S(2)}) %collective-permute-start.1) | collective-permute-done | bytes 393248 | tf_op jit(solution)/shard_map/ppermute | solution.py:19
  99.9 0.0 copy-done.1
  99.9 7.3 %diagrams.1 = (f32[6,2,128,128]{3,2,1,0:T(8,128)}, bf16[5,128,1536]{2,1,0:T(8,128)(2,1)S(1)}, bf16[5,384,1024]{2,1,0:T(8,128)(2,1)S(1)}) custom-call(s32[6,3]{1,0:T(8,128)S(1)} %bitcast.20, s32[1]{0:T(128)S(6)} %copy.25.count, s32[1]{0:T(128)} %bitcast.1.position, f32[2,4,4]{2,1,0:T(4,128)S(1)} %copy-done.3, ...), custom_call_target="tpu_custom_call", output_to_operand_aliasing={{1}: (8, {}), {2}: (9, {})} | custom-call | tf_op jit(solution)/shard_map/diagrams/pallas_call | solution.py:234
Async XLA Ops:
  0.0 11.2 %copy-start = (bf16[1,4,2,192,192]{4,3,2,1,0:T(8,128)(2,1)S(1)}, bf16[1,4,2,192,192]{4,3,2,1,0:T(8,128)(2,1)}, u32[]{:S(2)}) copy-start(bf16[1,4,2,192,192]{4,3,2,1,0:T(8,128)(2,1)} %param.8) | copy-start | bytes 1769476
  0.0 65.5 %all-to-all-start = ((bf16[1,16,2,48,768]{4,3,2,0,1:T(8,128)(2,1)}), bf16[1,16,2,48,768]{4,3,2,0,1:T(8,128)(2,1)S(1)}, u32[]{:S(2)}, u32[]{:S(2)}) async-start(bf16[1,16,2,48,768]{4,3,2,0,1:T(8,128)(2,1)} %bitcast.22), calls=%async_computation | async-start | bytes 4718592 | tf_op jit(solution)/shard_map/all_to_all | solution.py:176
  11.2 54.3 %copy-start.3 = (f32[2,4,4]{2,1,0:T(4,128)S(1)}, f32[2,4,4]{2,1,0:T(4,128)}, u32[]{:S(2)}) copy-start(f32[2,4,4]{2,1,0:T(4,128)} %gamma.3) | copy-start | bytes 388
  65.5 1.0 copy-start.2
  66.5 23.9 %copy-start.4 = (s32[1,6,3]{1,0,2:T(1,128)S(1)}, s32[1,6,3]{1,0,2:T(1,128)}, u32[]{:S(2)}) copy-start(s32[1,6,3]{1,0,2:T(1,128)} %param.11) | copy-start | bytes 220
  69.5 12.7 %collective-permute-start.2 = (bf16[2,768,128]{2,1,0:T(8,128)(2,1)S(1)}, bf16[2,768,128]{2,1,0:T(8,128)(2,1)S(1)}, u32[]{:S(2)}, u32[]{:S(2)}) collective-permute-start(bf16[2,768,128]{2,1,0:T(8,128)(2,1)S(1)} %dress.1.refs_2_), channel_id=1, source_target_pairs={{0,16},{32,48},{64,80},{96,112},{128,144},{160,176},{192,208},{224... | collective-permute-start | bytes 1179656 | tf_op jit(solution)/shard_map/ppermute | solution.py:19
  73.0 14.8 %collective-permute-start = (bf16[2,768,128]{2,1,0:T(8,128)(2,1)S(1)}, bf16[2,768,128]{2,1,0:T(8,128)(2,1)}, u32[]{:S(2)}, u32[]{:S(2)}) collective-permute-start(bf16[2,768,128]{2,1,0:T(8,128)(2,1)S(1)} %dress.1.refs_2_), channel_id=1, source_target_pairs={{16,32},{48,64},{80,96},{112,128},{144,160},{176,192},{208,224},{2... | collective-permute-start | bytes 1179656 | tf_op jit(solution)/shard_map/ppermute | solution.py:19
  82.2 14.0 %collective-permute-start.3 = (bf16[2,768,128]{2,1,0:T(8,128)(2,1)S(1)}, bf16[2,768,128]{2,1,0:T(8,128)(2,1)S(1)}, u32[]{:S(2)}, u32[]{:S(2)}) collective-permute-start(bf16[2,768,128]{2,1,0:T(8,128)(2,1)S(1)} %collective-permute-done.2.refs_2_), channel_id=1, source_target_pairs={{16,32},{48,64},{80,96},{112,128},{144,160},{176,192},{208,224},{2... | collective-permute-start | bytes 1179656 | tf_op jit(solution)/shard_map/ppermute | solution.py:19
  87.9 12.0 %collective-permute-start.1 = (bf16[2,768,128]{2,1,0:T(8,128)(2,1)}, bf16[2,768,128]{2,1,0:T(8,128)(2,1)}, u32[]{:S(2)}, u32[]{:S(2)}) collective-permute-start(bf16[2,768,128]{2,1,0:T(8,128)(2,1)} %collective-permute-done.refs_3_), channel_id=1, source_target_pairs={{0,16},{32,48},{64,80},{96,112},{128,144},{160,176},{192,208},{224... | collective-permute-start | bytes 1179656 | tf_op jit(solution)/shard_map/ppermute | solution.py:19
  92.5 7.3 %copy-start.1 = (bf16[4,192,384]{2,1,0:T(8,128)(2,1)S(1)}, bf16[4,192,384]{2,1,0:T(8,128)(2,1)}, u32[]{:S(2)}) copy-start(bf16[4,192,384]{2,1,0:T(8,128)(2,1)} %pad_maximum_fusion.backward) | copy-start | bytes 1769476

commit v3 on v2

--- a/solution.py
+++ b/solution.py
@@ -60,15 +60,18 @@
                 split[c, pl.ds(2 * half + q, nev, stride=4), :] = done[:, q * width : (q + 1) * width]
 
 
-def dress_kernel(ident, gamma, tau, sink, forward, out, split, mixed, matrix, rows, sem, *, depth):
+def left_kernel(sink, left, rows, *, depth):
+    stack_rows(sink[0], sink[1], rows, depth)
+    left[...] = rows[...].T
+
+
+def dress_kernel(ident, gamma, tau, left, table, out, split, mixed, matrix, sem):
     ndim, width = out.shape[1:]
     nev = ndim // 4
-    fetch = pltpu.make_async_copy(forward.at[ident[0]], matrix, sem)
+    fetch = pltpu.make_async_copy(table.at[ident[0]], matrix, sem)
     fetch.start()
-    stack_rows(sink[0], sink[1], rows, depth)
-    left = rows[...].T
     for at in range(0, ndim, 2 * width):
-        prop = dot(left, tau[:, at : at + 2 * width]).astype(BF).astype(F32)
+        prop = dot(left[...], tau[:, at : at + 2 * width]).astype(BF).astype(F32)
         split[0, at : at + 2 * width, :] = prop[:width].T
         split[1, at : at + 2 * width, :] = prop[width:].T
 
@@ -116,23 +119,40 @@
         wide[d, :, ndim + at : ndim + at + 2 * width] = product[width:]
 
 
-def prepare_kernel(*refs, depth, entries, fresh):
+def sort_kernel(tau, _, sorted_tau, order, chunk):
+    ndim = tau.shape[1]
+    nev = ndim // 4
+    row = lax.broadcasted_iota(jnp.int32, (ndim, nev), 0)
+    column = lax.broadcasted_iota(jnp.int32, (ndim, nev), 1)
+    for s in range(4):
+        order[:, s * nev : (s + 1) * nev] = (row == 4 * column + s).astype(F32).astype(BF)
+    for turn, at in enumerate(range(0, 2 * ndim, 256)):
+        chunk[turn % 2] = tau[at : at + 256, :]
+        sorted_tau[at : at + 256, :] = dot(chunk[turn % 2], order[...]).astype(BF)
+
+
+def own_kernel(gamma, tau, block, table, wide, mixed, fetched, rows, split, sem, *, depth):
+    fetch = pltpu.make_async_copy(table, fetched, sem)
+    fetch.start()
+    prepare(0, block, gamma, tau, wide, mixed, rows, split, depth)
+    fetch.wait()
+
+
+def prepare_kernel(*refs, depth, entries):
     gamma, tau = refs[:2]
     blocks = refs[2 : 2 + len(entries)]
-    rest = refs[2 + len(entries) + (0 if fresh else 2) :]
-    wide, mixed, rows, split = rest
+    wide, mixed, rows, split = refs[2 + len(entries) + 2 :]
     for turn, (d, block) in enumerate(zip(entries, blocks)):
         prepare(d, block, gamma, tau, wide, mixed, rows.at[turn], split.at[turn], depth)
 
 
 def diagrams_kernel(
-    lists, count, position, gamma, tau, low, high, backward, wide_in, mixed_in, out, wide, mixed,
-    rows, split, column, *, depth,
+    lists, count, position, gamma, tau, last, backward, wide_in, mixed_in, out, wide, mixed,
+    rows, split, column, totals, sem, *, depth,
 ):
-    ndim, width = low.shape[1:]
+    ndim, width = last.shape[1:]
     nev = ndim // 4
-    prepare(3, low, gamma, tau, wide, mixed, rows.at[0], split.at[0], depth)
-    prepare(4, high, gamma, tau, wide, mixed, rows.at[1], split.at[1], depth)
+    prepare(3, last, gamma, tau, wide, mixed, rows, split, depth)
     scale = (2.0 * ndim) ** (-0.5)
     here = position[0]
     sign = 1 - 2 * (here % 2)
@@ -146,23 +166,28 @@
     for k in range(out.shape[0]):
         first = entry(lists[k, 0])
         second = entry(lists[k, 1])
-        spread = split.at[k % 2]
-
-        def product(at):
-            return dot(backward[lists[k, 2]], mixed[first, :, at])
-
-        eigen_product(product, nev, spread, width)
-        u_r = spread[0].astype(BF)
-        u_i = spread[1].astype(BF)
         pair = column.at[k % 2]
-        pair[:ndim, :width] = u_r
-        pair[:ndim, width:] = u_i
-        pair[ndim:, :width] = u_i
-        pair[ndim:, width:] = -u_r
+        for half in range(2):
+            at = 2 * half * width
+            real = dot(backward[lists[k, 2]], mixed[first, :, at : at + 2 * width]).astype(BF)
+            at += 4 * width
+            imag = dot(backward[lists[k, 2]], mixed[first, :, at : at + 2 * width]).astype(BF)
+            for q in range(2):
+                s = 2 * half + q
+                part = slice(q * width, (q + 1) * width)
+                top = slice(s * nev, (s + 1) * nev)
+                low = slice(ndim + s * nev, ndim + (s + 1) * nev)
+                pair[top, :width] = real[:, part]
+                pair[top, width:] = imag[:, part]
+                pair[low, :width] = imag[:, part]
+                pair[low, width:] = -real[:, part]
         result = dot(wide[second], pair[...]) * scale
         result = jnp.where(k < count[0], result, 0.0)
-        out[k, 0] = result[:, :width]
-        out[k, 1] = result[:, width:]
+        totals[k, 0] = result[:, :width]
+        totals[k, 1] = result[:, width:]
+        pltpu.make_async_copy(totals.at[k], out.at[k], sem.at[k]).start()
+    for k in range(out.shape[0]):
+        pltpu.make_async_copy(totals.at[k], out.at[k], sem.at[k]).wait()
 
 
 def per_device(
@@ -179,19 +204,25 @@
     backward = jnp.concatenate(
         [jnp.swapaxes(table[:, 0], 1, 2), jnp.swapaxes(table[:, 1], 1, 2)], axis=2
     )
-    tau, backward = lax.optimization_barrier((tau, backward))
     smem = pl.BlockSpec(memory_space=pltpu.SMEM)
     vmem = pl.BlockSpec(memory_space=pltpu.VMEM)
     free = pl.BlockSpec(memory_space=pl.ANY)
-
-    def scratch(count):
-        return [
-            pltpu.VMEM((count, 2 * ndim, 2 * width), BF),
-            pltpu.VMEM((2, 2, ndim, width), F32),
-        ]
+    rows = pltpu.VMEM((2 * ndim, 2 * width), BF)
+    split = pltpu.VMEM((2, ndim, width), F32)
+    left = pl.pallas_call(
+        functools.partial(left_kernel, depth=depth),
+        out_shape=jax.ShapeDtypeStruct((2 * width, 2 * ndim), BF),
+        in_specs=[vmem],
+        out_specs=vmem,
+        scratch_shapes=[rows],
+        compiler_params=pltpu.CompilerParams(vmem_limit_bytes=6 << 20),
+        name="left",
+    )(sink_block)
+    tau, backward, left = lax.optimization_barrier((tau, backward, left))
+    backward = pltpu.with_memory_space_constraint(backward, pltpu.HBM)
 
     dressed = pl.pallas_call(
-        functools.partial(dress_kernel, depth=depth),
+        dress_kernel,
         out_shape=jax.ShapeDtypeStruct((2, ndim, width), BF),
         in_specs=[smem, smem, vmem, vmem, free],
         out_specs=vmem,
@@ -199,49 +230,77 @@
             pltpu.VMEM((2, ndim, width), F32),
             pltpu.VMEM((2 * nev, 8 * width), BF),
             pltpu.VMEM((2, nev, nev), BF),
-            pltpu.VMEM((2 * ndim, 2 * width), BF),
             pltpu.SemaphoreType.DMA,
         ],
         compiler_params=pltpu.CompilerParams(vmem_limit_bytes=10 << 20),
         name="dress",
-    )(source_ids, gamma_spin, tau, sink_block, table)
+    )(source_ids, gamma_spin, tau, left, pltpu.with_memory_space_constraint(table, pltpu.HBM))
     state = (
         jax.ShapeDtypeStruct((reach, width, 2 * ndim), BF),
         jax.ShapeDtypeStruct((reach, 2 * nev, 8 * width), BF),
     )
 
-    def prepared(blocks, entries, held=()):
-        fresh = not held
+
+    def prepared(blocks, entries, held):
         count = 2 + len(blocks)
         return pl.pallas_call(
-            functools.partial(prepare_kernel, depth=depth, entries=entries, fresh=fresh),
+            functools.partial(prepare_kernel, depth=depth, entries=entries),
             out_shape=state,
             in_specs=[smem, vmem] + [vmem] * (len(blocks) + len(held)),
             out_specs=(vmem, vmem),
-            scratch_shapes=scratch(len(blocks)),
-            input_output_aliases={} if fresh else {count: 0, count + 1: 1},
+            scratch_shapes=[
+                pltpu.VMEM((len(blocks), *rows.shape), BF),
+                pltpu.VMEM((len(blocks), *split.shape), F32),
+            ],
+            input_output_aliases={count: 0, count + 1: 1},
             compiler_params=pltpu.CompilerParams(vmem_limit_bytes=12 << 20),
             name="prepare",
         )(gamma_spin, tau, *blocks, *held)
 
     even = swapped(dressed, "src", 0)
     odd = swapped(dressed, "src", 1)
-    held = prepared((dressed,), (0,))
+    tau = pl.pallas_call(
+        sort_kernel,
+        out_shape=jax.ShapeDtypeStruct(tau.shape, BF),
+        in_specs=[vmem, free],
+        out_specs=vmem,
+        scratch_shapes=[pltpu.VMEM((ndim, ndim), BF), pltpu.VMEM((2, 256, ndim), BF)],
+        compiler_params=pltpu.CompilerParams(vmem_limit_bytes=8 << 20),
+        input_output_aliases={0: 0},
+        name="sort",
+    )(tau, dressed)
+    even, tau = lax.optimization_barrier((even, tau))
     odd_far = swapped(even, "src", 1)
     even_far = swapped(odd, "src", 0)
+    *held, backward = pl.pallas_call(
+        functools.partial(own_kernel, depth=depth),
+        out_shape=(*state, jax.ShapeDtypeStruct(backward.shape, BF)),
+        in_specs=[smem, vmem, vmem, free],
+        out_specs=(vmem, vmem, vmem),
+        scratch_shapes=[rows, split, pltpu.SemaphoreType.DMA],
+        compiler_params=pltpu.CompilerParams(vmem_limit_bytes=12 << 20),
+        name="own",
+    )(gamma_spin, tau, dressed, backward)
     held = prepared((even, odd), (1, 2), held)
+    held = prepared((odd_far,), (4,), held)
     position = lax.axis_index("src").astype(jnp.int32).reshape(1)
     totals, _, _ = pl.pallas_call(
         functools.partial(diagrams_kernel, depth=depth),
         out_shape=(jax.ShapeDtypeStruct((slots, 2, width, width), F32), *state),
-        in_specs=[smem] * 4 + [vmem] * 6,
-        out_specs=(vmem, vmem, vmem),
-        scratch_shapes=scratch(2) + [pltpu.VMEM((2, 2 * ndim, 2 * width), BF)],
-        input_output_aliases={8: 1, 9: 2},
+        in_specs=[smem] * 4 + [vmem] * 5,
+        out_specs=(free, vmem, vmem),
+        scratch_shapes=[
+            rows,
+            split,
+            pltpu.VMEM((2, 2 * ndim, 2 * width), BF),
+            pltpu.VMEM((slots, 2, width, width), F32),
+            pltpu.SemaphoreType.DMA((slots,)),
+        ],
+        input_output_aliases={7: 1, 8: 2},
         compiler_params=pltpu.CompilerParams(vmem_limit_bytes=16 << 20),
         name="diagrams",
     )(
-        graph_lists[0], diagram_counts, position, gamma_spin, tau, even_far, odd_far, backward, *held
+        graph_lists[0], diagram_counts, position, gamma_spin, tau, even_far, backward, *held
     )
     return totals[None, None]
 

time: 108 us -> 105 us (0.972)
  waiting for transfers between devices: 58.4 us -> 52.6 us
  Pallas kernels: 15.8 us -> 19.5 us
    ppermute x4, waiting for transfers between devices: 7.56 us -> 2.06 us  [swapped(): lax.ppermute(shard, axis, [(i, i + 1) for i in lower] + [(i + 1, i) for i...]
    pallas_call x1 -> x4, Pallas kernels: 3.02 us -> 8.42 us  [the longest x1 3.5 us: per_device(): pl.pallas_call(dress_kernel, out_shape=jax.ShapeDtypeStruct((2, ndim, wid...]
    pallas_call x1, Pallas kernels: 7.3 us -> 5.22 us  [per_device(): pl.pallas_call(functools.partial(diagrams_kernel, depth=depth), out_shape...]
    unnamed x11 -> x9, local copies, waits for them, and re-layouts: 2.24 us -> 1.24 us
  transfers between devices with their start and end apart: 5 -> 5, of which waited for: 4 -> 4; matrix products, arithmetic and copies ran while one was open for 3% -> 3% of each run, Pallas kernels for 5% -> 10%
where the time goes in v3:
time: 105 us; the launch traced here: 104 us
  waiting for transfers between devices  52.6 us (50%)
  starting transfers between devices  27.2 us (26%)
  Pallas kernels  19.5 us (19%)
  local copies, waits for them, and re-layouts  2.5 us (2%)
  between operations  1.59 us (2%)
    all_to_all x1, waiting for transfers between devices, per_device(): lax.all_to_all(perambulator, 'col', split_axis=1, concat_axis=1, tiled=True)  50.6 us
    ppermute x4, starting transfers between devices, swapped(): lax.ppermute(shard, axis, [(i, i + 1) for i in lower] + [(i + 1, i) for i...  16.6 us
    all_to_all x1, starting transfers between devices, per_device(): lax.all_to_all(perambulator, 'col', split_axis=1, concat_axis=1, tiled=True)  10.6 us
    pallas_call x2, Pallas kernels, prepared(): pl.pallas_call(functools.partial(prepare_kernel, depth=depth, entries=ent...  5.84 us
    pallas_call x1, Pallas kernels, per_device(): pl.pallas_call(functools.partial(diagrams_kernel, depth=depth), out_shape...  5.22 us
    pallas_call x1, Pallas kernels, per_device(): pl.pallas_call(dress_kernel, out_shape=jax.ShapeDtypeStruct((2, ndim, wid...  3.5 us
    pallas_call x1, Pallas kernels, per_device(): pl.pallas_call(sort_kernel, out_shape=jax.ShapeDtypeStruct(tau.shape, BF)...  2.53 us
    pallas_call x1, Pallas kernels, per_device(): pl.pallas_call(functools.partial(own_kernel, depth=depth), out_shape=(*st...  2.12 us
  transfers between devices with their start and end apart: 5, of which 4 were waited for; matrix products, arithmetic and copies ran while one was open for 3% of the time, Pallas kernels for 10%

profile of v3, /device:TPU:6, one launch (start us, length us, event | category | flops | bytes accessed | tf_op | source)
XLA Modules:
  0.0 104.4 jit_solution(3255617946403245712)
XLA Ops:
  0.0 0.0 copy-start.2
  0.0 0.0 copy-start
  0.0 10.6 %all-to-all-start = ((bf16[1,16,2,48,768]{4,3,2,0,1:T(8,128)(2,1)}), bf16[1,16,2,48,768]{4,3,2,0,1:T(8,128)(2,1)S(1)}, u32[]{:S(2)}, u32[]{:S(2)}) async-start(bf16[1,16,2,48,768]{4,3,2,0,1:T(8,128)(2,1)} %bitcast.20), calls=%async_computation | async-start | bytes 4718592 | tf_op jit(solution)/shard_map/all_to_all | solution.py:201
  10.6 0.0 copy-done.2
  10.6 1.2 %copy.19 = bf16[1,4,2,192,192]{3,4,1,2,0:T(8,128)(2,1)} copy(bf16[1,4,2,192,192]{4,3,2,1,0:T(8,128)(2,1)S(1)} %copy-done.2) | data formatting | bytes 1179648 | tf_op args[1]
  11.8 0.0 copy-done
  11.8 0.0 copy-start.1
  11.8 0.3 left.1
  12.7 1.2 %slice_bitcast_fusion.1 = (bf16[4,192,192]{2,1,0:T(8,128)(2,1)S(1)}, bf16[4,192,192]{2,1,0:T(8,128)(2,1)S(1)}) fusion(bf16[4,2,192,192]{2,3,0,1:T(8,128)(2,1)} %bitcast.18), kind=kLoop, calls=%fused_computation.2 | loop fusion | bytes 1179648 | tf_op jit(solution)/shard_map/transpose | solution.py:205
  13.9 1.0 pad_maximum_fusion.table
  14.9 50.6 %all-to-all-done = bf16[1,16,2,48,768]{4,3,2,0,1:T(8,128)(2,1)S(1)} async-done(((bf16[1,16,2,48,768]{4,3,2,0,1:T(8,128)(2,1)}), bf16[1,16,2,48,768]{4,3,2,0,1:T(8,128)(2,1)S(1)}, u32[]{:S(2)}, u32[]{:S(2)}) %all-to-all-start) | async-done | bytes 2359328 | tf_op jit(solution)/shard_map/all_to_all | solution.py:201
  65.5 0.0 copy-done.1
  65.5 3.5 %dress.1._.block = bf16[2,768,128]{2,1,0:T(8,128)(2,1)S(1)} custom-call(s32[1]{0:T(128)S(6)} %copy.32.ident, f32[2,4,4]{2,1,0:T(4,128)S(1)} %copy-done.1, bf16[1536,768]{1,0:T(8,128)(2,1)S(1)} %bitcast.15, bf16[256,1536]{1,0:T(8,128)(2,1)S(1)} %left.1, bf16[4,2,192,192]{3,2,1,0:T(8,128)(2,1)} %bitcast.19), custom_call_target="tpu_custom_call" | custom-call | tf_op jit(solution)/shard_map/dress/pallas_call | solution.py:224
  69.0 0.0 copy-start.3
  69.0 3.5 %collective-permute-start = (bf16[2,768,128]{2,1,0:T(8,128)(2,1)S(1)}, bf16[2,768,128]{2,1,0:T(8,128)(2,1)}, u32[]{:S(2)}, u32[]{:S(2)}) collective-permute-start(bf16[2,768,128]{2,1,0:T(8,128)(2,1)S(1)} %dress.1._.block), channel_id=1, source_target_pairs={{0,16},{32,48},{64,80},{96,112},{128,144},{160,176},{192,208},{224... | collective-permute-start | bytes 1179656 | tf_op jit(solution)/shard_map/ppermute | solution.py:19
  72.5 5.4 %collective-permute-start.1 = (bf16[2,768,128]{2,1,0:T(8,128)(2,1)S(1)}, bf16[2,768,128]{2,1,0:T(8,128)(2,1)S(1)}, u32[]{:S(2)}, u32[]{:S(2)}) collective-permute-start(bf16[2,768,128]{2,1,0:T(8,128)(2,1)S(1)} %dress.1._.block), channel_id=1, source_target_pairs={{16,32},{48,64},{80,96},{112,128},{144,160},{176,192},{208,224},{2... | collective-permute-start | bytes 1179656 | tf_op jit(solution)/shard_map/ppermute | solution.py:19
  78.0 2.5 %sort.1.tau.refs_1_ = bf16[1536,768]{1,0:T(8,128)(2,1)S(1)} custom-call(bf16[1536,768]{1,0:T(8,128)(2,1)S(1)} %bitcast.16, bf16[2,768,128]{2,1,0:T(8,128)(2,1)S(1)} %dress.1._.block), custom_call_target="tpu_custom_call", output_to_operand_aliasing={{}: (0, {})} | custom-call | tf_op jit(solution)/shard_map/sort/pallas_call | solution.py:262
  80.5 1.4 %collective-permute-done.refs_2_ = bf16[2,768,128]{2,1,0:T(8,128)(2,1)} collective-permute-done((bf16[2,768,128]{2,1,0:T(8,128)(2,1)S(1)}, bf16[2,768,128]{2,1,0:T(8,128)(2,1)}, u32[]{:S(2)}, u32[]{:S(2)}) %collective-permute-start) | collective-permute-done | bytes 393248 | tf_op jit(solution)/shard_map/ppermute | solution.py:19
  81.8 5.6 %collective-permute-start.3 = (bf16[2,768,128]{2,1,0:T(8,128)(2,1)}, bf16[2,768,128]{2,1,0:T(8,128)(2,1)}, u32[]{:S(2)}, u32[]{:S(2)}) collective-permute-start(bf16[2,768,128]{2,1,0:T(8,128)(2,1)} %collective-permute-done.refs_2_), channel_id=1, source_target_pairs={{16,32},{48,64},{80,96},{112,128},{144,160},{176,192},{208,224},{2... | collective-permute-start | bytes 1179656 | tf_op jit(solution)/shard_map/ppermute | solution.py:19
  87.5 0.0 collective-permute-done.1.refs_3_
  87.5 2.1 %collective-permute-start.2 = (bf16[2,768,128]{2,1,0:T(8,128)(2,1)S(1)}, bf16[2,768,128]{2,1,0:T(8,128)(2,1)S(1)}, u32[]{:S(2)}, u32[]{:S(2)}) collective-permute-start(bf16[2,768,128]{2,1,0:T(8,128)(2,1)S(1)} %collective-permute-done.1.refs_3_), channel_id=1, source_target_pairs={{0,16},{32,48},{64,80},{96,112},{128,144},{160,176},{192,208},{224... | collective-permute-start | bytes 1179656 | tf_op jit(solution)/shard_map/ppermute | solution.py:19
  89.6 0.0 copy-done.3
  89.6 0.1 copy.22
  90.4 2.1 %own.1 = (bf16[5,128,1536]{2,1,0:T(8,128)(2,1)S(1)}, bf16[5,384,1024]{2,1,0:T(8,128)(2,1)S(1)}, bf16[4,192,384]{2,1,0:T(8,128)(2,1)S(1)}) custom-call(f32[2,4,4]{2,1,0:T(4,128)S(1)} %copy-done.1, bf16[1536,768]{1,0:T(8,128)(2,1)S(1)} %sort.1.tau.refs_1_, bf16[2,768,128]{2,1,0:T(8,128)(2,1)S(1)} %dress.1._.block, bf16[4,192,384]{2,1,0:T(8,128)(2,1)} %pad_maximum_fusion.table), custom_call_target="tpu_custom_call" | custom-call | tf_op jit(solution)/shard_map/own/pallas_call | solution.py:275
  92.5 3.5 %prepare.2 = (bf16[5,128,1536]{2,1,0:T(8,128)(2,1)S(1)}, bf16[5,384,1024]{2,1,0:T(8,128)(2,1)S(1)}) custom-call(f32[2,4,4]{2,1,0:T(4,128)S(1)} %copy-done.1, bf16[1536,768]{1,0:T(8,128)(2,1)S(1)} %sort.1.tau.refs_1_, bf16[2,768,128]{2,1,0:T(8,128)(2,1)} %collective-permute-done.refs_2_, ...), custom_call_target="tpu_custom_call", output_to_operand_aliasing={{0}: (4, {}), {1}: (5, {})} | custom-call | tf_op jit(solution)/shard_map/prepare/pallas_call | solution.py:246
  96.0 0.1 collective-permute-done.3.refs_2_
  96.1 2.4 %prepare.3 = (bf16[5,128,1536]{2,1,0:T(8,128)(2,1)S(1)}, bf16[5,384,1024]{2,1,0:T(8,128)(2,1)S(1)}) custom-call(f32[2,4,4]{2,1,0:T(4,128)S(1)} %copy-done.1, bf16[1536,768]{1,0:T(8,128)(2,1)S(1)} %sort.1.tau.refs_1_, bf16[2,768,128]{2,1,0:T(8,128)(2,1)} %collective-permute-done.3.refs_2_, ...), custom_call_target="tpu_custom_call", output_to_operand_aliasing={{0}: (3, {}), {1}: (4, {})} | custom-call | tf_op jit(solution)/shard_map/prepare/pallas_call | solution.py:246
  98.5 0.6 collective-permute-done.2.last
  99.1 5.2 %diagrams.1 = (f32[6,2,128,128]{3,2,1,0:T(8,128)}, bf16[5,128,1536]{2,1,0:T(8,128)(2,1)S(1)}, bf16[5,384,1024]{2,1,0:T(8,128)(2,1)S(1)}) custom-call(s32[6,3]{1,0:T(8,128)S(1)} %bitcast.17, s32[1]{0:T(128)S(6)} %copy.31.count, s32[1]{0:T(128)} %bitcast.1.position, f32[2,4,4]{2,1,0:T(4,128)S(1)} %copy-done.1, ...), custom_call_target="tpu_custom_call", output_to_operand_aliasing={{1}: (7, {}), {2}: (8, {})} | custom-call | tf_op jit(solution)/shard_map/diagrams/pallas_call | solution.py:287
Async XLA Ops:
  0.0 10.6 %copy-start.2 = (bf16[1,4,2,192,192]{4,3,2,1,0:T(8,128)(2,1)S(1)}, bf16[1,4,2,192,192]{4,3,2,1,0:T(8,128)(2,1)}, u32[]{:S(2)}) copy-start(bf16[1,4,2,192,192]{4,3,2,1,0:T(8,128)(2,1)} %param.8) | copy-start | bytes 1769476
  0.0 11.8 %copy-start = (bf16[2,768,128]{2,1,0:T(8,128)(2,1)S(1)}, bf16[2,768,128]{2,1,0:T(8,128)(2,1)}, u32[]{:S(2)}) copy-start(bf16[2,768,128]{2,1,0:T(8,128)(2,1)} %sink.1) | copy-start | bytes 1179652
  0.0 65.5 %all-to-all-start = ((bf16[1,16,2,48,768]{4,3,2,0,1:T(8,128)(2,1)}), bf16[1,16,2,48,768]{4,3,2,0,1:T(8,128)(2,1)S(1)}, u32[]{:S(2)}, u32[]{:S(2)}) async-start(bf16[1,16,2,48,768]{4,3,2,0,1:T(8,128)(2,1)} %bitcast.20), calls=%async_computation | async-start | bytes 4718592 | tf_op jit(solution)/shard_map/all_to_all | solution.py:201
  11.8 53.7 %copy-start.1 = (f32[2,4,4]{2,1,0:T(4,128)S(1)}, f32[2,4,4]{2,1,0:T(4,128)}, u32[]{:S(2)}) copy-start(f32[2,4,4]{2,1,0:T(4,128)} %gamma.5) | copy-start | bytes 388
  69.0 20.6 %copy-start.3 = (s32[1,6,3]{1,0,2:T(1,128)S(1)}, s32[1,6,3]{1,0,2:T(1,128)}, u32[]{:S(2)}) copy-start(s32[1,6,3]{1,0,2:T(1,128)} %param.11) | copy-start | bytes 220
  69.0 12.8 %collective-permute-start = (bf16[2,768,128]{2,1,0:T(8,128)(2,1)S(1)}, bf16[2,768,128]{2,1,0:T(8,128)(2,1)}, u32[]{:S(2)}, u32[]{:S(2)}) collective-permute-start(bf16[2,768,128]{2,1,0:T(8,128)(2,1)S(1)} %dress.1._.block), channel_id=1, source_target_pairs={{0,16},{32,48},{64,80},{96,112},{128,144},{160,176},{192,208},{224... | collective-permute-start | bytes 1179656 | tf_op jit(solution)/shard_map/ppermute | solution.py:19
  72.5 15.0 %collective-permute-start.1 = (bf16[2,768,128]{2,1,0:T(8,128)(2,1)S(1)}, bf16[2,768,128]{2,1,0:T(8,128)(2,1)S(1)}, u32[]{:S(2)}, u32[]{:S(2)}) collective-permute-start(bf16[2,768,128]{2,1,0:T(8,128)(2,1)S(1)} %dress.1._.block), channel_id=1, source_target_pairs={{16,32},{48,64},{80,96},{112,128},{144,160},{176,192},{208,224},{2... | collective-permute-start | bytes 1179656 | tf_op jit(solution)/shard_map/ppermute | solution.py:19
  81.8 14.3 %collective-permute-start.3 = (bf16[2,768,128]{2,1,0:T(8,128)(2,1)}, bf16[2,768,128]{2,1,0:T(8,128)(2,1)}, u32[]{:S(2)}, u32[]{:S(2)}) collective-permute-start(bf16[2,768,128]{2,1,0:T(8,128)(2,1)} %collective-permute-done.refs_2_), channel_id=1, source_target_pairs={{16,32},{48,64},{80,96},{112,128},{144,160},{176,192},{208,224},{2... | collective-permute-start | bytes 1179656 | tf_op jit(solution)/shard_map/ppermute | solution.py:19
  87.5 11.6 %collective-permute-start.2 = (bf16[2,768,128]{2,1,0:T(8,128)(2,1)S(1)}, bf16[2,768,128]{2,1,0:T(8,128)(2,1)S(1)}, u32[]{:S(2)}, u32[]{:S(2)}) collective-permute-start(bf16[2,768,128]{2,1,0:T(8,128)(2,1)S(1)} %collective-permute-done.1.refs_3_), channel_id=1, source_target_pairs={{0,16},{32,48},{64,80},{96,112},{128,144},{160,176},{192,208},{224... | collective-permute-start | bytes 1179656 | tf_op jit(solution)/shard_map/ppermute | solution.py:19

commit v4 on v3

--- a/solution.py
+++ b/solution.py
@@ -40,12 +40,13 @@
         for s in range(4):
             real = imag = None
             for q in range(4):
-                if adjoint:
-                    g_r, g_i = gamma[0, q, s], -gamma[1, q, s]
-                else:
-                    g_r, g_i = gamma[0, s, q], gamma[1, s, q]
-                term_r = g_r * part[0][q] - g_i * part[1][q]
-                term_i = g_r * part[1][q] + g_i * part[0][q]
+                at = 4 * q + s if adjoint else 4 * s + q
+                g_r = gamma[pl.ds(at, TILE, stride=0), :]
+                g_i = gamma[pl.ds(16 + at, TILE, stride=0), :]
+                cross_r = g_i * part[1][q]
+                cross_i = g_i * part[0][q]
+                term_r = g_r * part[0][q] + cross_r if adjoint else g_r * part[0][q] - cross_r
+                term_i = g_r * part[1][q] - cross_i if adjoint else g_r * part[1][q] + cross_i
                 real = term_r if real is None else real + term_r
                 imag = term_i if imag is None else imag + term_i
             write(start, s, real, imag)
@@ -60,18 +61,20 @@
                 split[c, pl.ds(2 * half + q, nev, stride=4), :] = done[:, q * width : (q + 1) * width]
 
 
-def left_kernel(sink, left, rows, *, depth):
+def left_kernel(ident, sink, table, left, rows, *, depth):
+    nev = table.shape[3]
     stack_rows(sink[0], sink[1], rows, depth)
-    left[...] = rows[...].T
-
-
-def dress_kernel(ident, gamma, tau, left, table, out, split, mixed, matrix, sem):
+    left[:, : rows.shape[0]] = rows[...].T
+    for c in range(2):
+        at = rows.shape[0] + c * 256
+        left[:nev, at : at + nev] = table[ident[0], c]
+
+
+def dress_kernel(gamma, tau, left, out, split, mixed):
     ndim, width = out.shape[1:]
     nev = ndim // 4
-    fetch = pltpu.make_async_copy(table.at[ident[0]], matrix, sem)
-    fetch.start()
     for at in range(0, ndim, 2 * width):
-        prop = dot(left[...], tau[:, at : at + 2 * width]).astype(BF).astype(F32)
+        prop = dot(left[:, : 2 * ndim], tau[:, at : at + 2 * width]).astype(BF).astype(F32)
         split[0, at : at + 2 * width, :] = prop[:width].T
         split[1, at : at + 2 * width, :] = prop[width:].T
 
@@ -86,10 +89,11 @@
         mixed[low, at_i] = real.astype(BF)
 
     spin_mix(split, gamma, False, write, range(0, nev, TILE))
-    fetch.wait()
+    real = left[:nev, 2 * ndim : 2 * ndim + nev]
+    imag = left[:nev, 2 * ndim + 256 : 2 * ndim + 256 + nev]
 
     def product(at):
-        return dot(matrix[0], mixed[:nev, at]) + dot(matrix[1], mixed[nev:, at])
+        return dot(real, mixed[:nev, at]) + dot(imag, mixed[nev:, at])
 
     eigen_product(product, nev, split, width)
     out[...] = split[...].astype(BF)
@@ -147,14 +151,14 @@
 
 
 def diagrams_kernel(
-    lists, count, position, gamma, tau, last, backward, wide_in, mixed_in, out, wide, mixed,
+    meta, gamma, tau, last, backward, wide_in, mixed_in, out, wide, mixed,
     rows, split, column, totals, sem, *, depth,
 ):
     ndim, width = last.shape[1:]
     nev = ndim // 4
     prepare(3, last, gamma, tau, wide, mixed, rows, split, depth)
     scale = (2.0 * ndim) ** (-0.5)
-    here = position[0]
+    here = meta[meta.shape[0] - 1]
     sign = 1 - 2 * (here % 2)
 
     def entry(sender):
@@ -164,14 +168,14 @@
         return jnp.where(ahead == 0, 0, jnp.where(ahead * ahead == 1, near, far))
 
     for k in range(out.shape[0]):
-        first = entry(lists[k, 0])
-        second = entry(lists[k, 1])
+        first = entry(meta[3 * k])
+        second = entry(meta[3 * k + 1])
         pair = column.at[k % 2]
         for half in range(2):
             at = 2 * half * width
-            real = dot(backward[lists[k, 2]], mixed[first, :, at : at + 2 * width]).astype(BF)
+            real = dot(backward[meta[3 * k + 2]], mixed[first, :, at : at + 2 * width]).astype(BF)
             at += 4 * width
-            imag = dot(backward[lists[k, 2]], mixed[first, :, at : at + 2 * width]).astype(BF)
+            imag = dot(backward[meta[3 * k + 2]], mixed[first, :, at : at + 2 * width]).astype(BF)
             for q in range(2):
                 s = 2 * half + q
                 part = slice(q * width, (q + 1) * width)
@@ -182,7 +186,7 @@
                 pair[low, :width] = imag[:, part]
                 pair[low, width:] = -real[:, part]
         result = dot(wide[second], pair[...]) * scale
-        result = jnp.where(k < count[0], result, 0.0)
+        result = jnp.where(k < meta[meta.shape[0] - 2], result, 0.0)
         totals[k, 0] = result[:, :width]
         totals[k, 1] = result[:, width:]
         pltpu.make_async_copy(totals.at[k], out.at[k], sem.at[k]).start()
@@ -211,30 +215,31 @@
     split = pltpu.VMEM((2, ndim, width), F32)
     left = pl.pallas_call(
         functools.partial(left_kernel, depth=depth),
-        out_shape=jax.ShapeDtypeStruct((2 * width, 2 * ndim), BF),
-        in_specs=[vmem],
+        out_shape=jax.ShapeDtypeStruct((2 * width, 2 * ndim + 512), BF),
+        in_specs=[smem, vmem, vmem],
         out_specs=vmem,
         scratch_shapes=[rows],
-        compiler_params=pltpu.CompilerParams(vmem_limit_bytes=6 << 20),
+        compiler_params=pltpu.CompilerParams(vmem_limit_bytes=8 << 20),
         name="left",
-    )(sink_block)
-    tau, backward, left = lax.optimization_barrier((tau, backward, left))
+    )(source_ids, sink_block, table)
+    gamma = jnp.broadcast_to(gamma_spin.reshape(-1, 1), (gamma_spin.size, width))
+    position = lax.axis_index("src").astype(jnp.int32).reshape(1)
+    meta = jnp.concatenate([graph_lists.reshape(-1), diagram_counts, position])
+    tau, backward, left, gamma, meta = lax.optimization_barrier((tau, backward, left, gamma, meta))
     backward = pltpu.with_memory_space_constraint(backward, pltpu.HBM)
 
     dressed = pl.pallas_call(
         dress_kernel,
         out_shape=jax.ShapeDtypeStruct((2, ndim, width), BF),
-        in_specs=[smem, smem, vmem, vmem, free],
+        in_specs=[vmem, vmem, vmem],
         out_specs=vmem,
         scratch_shapes=[
             pltpu.VMEM((2, ndim, width), F32),
             pltpu.VMEM((2 * nev, 8 * width), BF),
-            pltpu.VMEM((2, nev, nev), BF),
-            pltpu.SemaphoreType.DMA,
         ],
         compiler_params=pltpu.CompilerParams(vmem_limit_bytes=10 << 20),
         name="dress",
-    )(source_ids, gamma_spin, tau, left, pltpu.with_memory_space_constraint(table, pltpu.HBM))
+    )(gamma, tau, left)
     state = (
         jax.ShapeDtypeStruct((reach, width, 2 * ndim), BF),
         jax.ShapeDtypeStruct((reach, 2 * nev, 8 * width), BF),
@@ -246,7 +251,7 @@
         return pl.pallas_call(
             functools.partial(prepare_kernel, depth=depth, entries=entries),
             out_shape=state,
-            in_specs=[smem, vmem] + [vmem] * (len(blocks) + len(held)),
+            in_specs=[vmem] * (2 + len(blocks) + len(held)),
             out_specs=(vmem, vmem),
             scratch_shapes=[
                 pltpu.VMEM((len(blocks), *rows.shape), BF),
@@ -255,7 +260,7 @@
             input_output_aliases={count: 0, count + 1: 1},
             compiler_params=pltpu.CompilerParams(vmem_limit_bytes=12 << 20),
             name="prepare",
-        )(gamma_spin, tau, *blocks, *held)
+        )(gamma, tau, *blocks, *held)
 
     even = swapped(dressed, "src", 0)
     odd = swapped(dressed, "src", 1)
@@ -275,19 +280,18 @@
     *held, backward = pl.pallas_call(
         functools.partial(own_kernel, depth=depth),
         out_shape=(*state, jax.ShapeDtypeStruct(backward.shape, BF)),
-        in_specs=[smem, vmem, vmem, free],
+        in_specs=[vmem, vmem, vmem, free],
         out_specs=(vmem, vmem, vmem),
         scratch_shapes=[rows, split, pltpu.SemaphoreType.DMA],
         compiler_params=pltpu.CompilerParams(vmem_limit_bytes=12 << 20),
         name="own",
-    )(gamma_spin, tau, dressed, backward)
+    )(gamma, tau, dressed, backward)
     held = prepared((even, odd), (1, 2), held)
     held = prepared((odd_far,), (4,), held)
-    position = lax.axis_index("src").astype(jnp.int32).reshape(1)
     totals, _, _ = pl.pallas_call(
         functools.partial(diagrams_kernel, depth=depth),
         out_shape=(jax.ShapeDtypeStruct((slots, 2, width, width), F32), *state),
-        in_specs=[smem] * 4 + [vmem] * 5,
+        in_specs=[smem] + [vmem] * 6,
         out_specs=(free, vmem, vmem),
         scratch_shapes=[
             rows,
@@ -296,11 +300,11 @@
             pltpu.VMEM((slots, 2, width, width), F32),
             pltpu.SemaphoreType.DMA((slots,)),
         ],
-        input_output_aliases={7: 1, 8: 2},
+        input_output_aliases={5: 1, 6: 2},
         compiler_params=pltpu.CompilerParams(vmem_limit_bytes=16 << 20),
         name="diagrams",
     )(
-        graph_lists[0], diagram_counts, position, gamma_spin, tau, even_far, backward, *held
+        meta, gamma, tau, even_far, backward, *held
     )
     return totals[None, None]
 

time: 105 us -> 103 us (0.981)
  Pallas kernels: 19.5 us -> 14.8 us
  local copies, waits for them, and re-layouts: 2.5 us -> 4.48 us
    ppermute x4, waiting for transfers between devices: 2.06 us -> 5.62 us  [swapped(): lax.ppermute(shard, axis, [(i, i + 1) for i in lower] + [(i + 1, i) for i...]
    unnamed x9 -> x14, local copies, waits for them, and re-layouts: 1.24 us -> 4.19 us
    all_to_all x1, waiting for transfers between devices: 50.6 us -> 47.8 us  [per_device(): lax.all_to_all(perambulator, 'col', split_axis=1, concat_axis=1, tiled=True)]
    pallas_call x2, Pallas kernels: 5.84 us -> 3.74 us  [prepared(): pl.pallas_call(functools.partial(prepare_kernel, depth=depth, entries=ent...]
    pallas_call x1, Pallas kernels: 3.5 us -> 1.92 us  [per_device(): pl.pallas_call(dress_kernel, out_shape=jax.ShapeDtypeStruct((2, ndim, wid...]
    transpose x1, local copies, waits for them, and re-layouts: 1.17 us -> 0.05 us  [per_device(): jnp.swapaxes(table[:, 0], 1, 2)]
  transfers between devices with their start and end apart: 5 -> 5, of which waited for: 4 -> 4; matrix products, arithmetic and copies ran while one was open for 3% -> 3% of each run, Pallas kernels for 10% -> 8%
where the time goes in v4:
time: 103 us
  waiting for transfers between devices  53.4 us (52%)
  starting transfers between devices  27.2 us (26%)
  Pallas kernels  14.8 us (14%)
  local copies, waits for them, and re-layouts  4.48 us (4%)
  between operations  1.61 us (2%)
  other arithmetic  1.11 us (1%)
    all_to_all x1, waiting for transfers between devices, per_device(): lax.all_to_all(perambulator, 'col', split_axis=1, concat_axis=1, tiled=True)  47.8 us
    ppermute x4, starting transfers between devices, swapped(): lax.ppermute(shard, axis, [(i, i + 1) for i in lower] + [(i + 1, i) for i...  16.6 us
    all_to_all x1, starting transfers between devices, per_device(): lax.all_to_all(perambulator, 'col', split_axis=1, concat_axis=1, tiled=True)  10.6 us
    ppermute x4, waiting for transfers between devices, swapped(): lax.ppermute(shard, axis, [(i, i + 1) for i in lower] + [(i + 1, i) for i...  5.62 us
    pallas_call x1, Pallas kernels, per_device(): pl.pallas_call(functools.partial(diagrams_kernel, depth=depth), out_shape...  5.03 us
    unnamed x14, local copies, waits for them, and re-layouts  4.19 us
    pallas_call x2, Pallas kernels, prepared(): pl.pallas_call(functools.partial(prepare_kernel, depth=depth, entries=ent...  3.74 us
    pallas_call x1, Pallas kernels, per_device(): pl.pallas_call(sort_kernel, out_shape=jax.ShapeDtypeStruct(tau.shape, BF)...  2.53 us
  transfers between devices with their start and end apart: 5, of which 4 were waited for; matrix products, arithmetic and copies ran while one was open for 3% of the time, Pallas kernels for 8%

profile of v4, /device:TPU:6, one launch (start us, length us, event | category | flops | bytes accessed | tf_op | source)
XLA Modules:
  0.0 102.6 jit_solution(15812887201713527517)
XLA Ops:
  0.0 0.0 copy-start
  0.0 0.0 copy-start.4
  0.0 0.0 copy-start.5
  0.0 10.6 %all-to-all-start = ((bf16[1,16,2,48,768]{4,3,2,0,1:T(8,128)(2,1)}), bf16[1,16,2,48,768]{4,3,2,0,1:T(8,128)(2,1)S(1)}, u32[]{:S(2)}, u32[]{:S(2)}) async-start(bf16[1,16,2,48,768]{4,3,2,0,1:T(8,128)(2,1)} %bitcast.18), calls=%async_computation | async-start | bytes 4718592 | tf_op jit(solution)/shard_map/all_to_all | solution.py:205
  10.6 0.0 copy-done
  10.6 1.2 %copy.22 = bf16[1,4,2,192,192]{3,4,1,2,0:T(8,128)(2,1)} copy(bf16[1,4,2,192,192]{4,3,2,1,0:T(8,128)(2,1)S(1)} %copy-done) | data formatting | bytes 1179648 | tf_op args[1]
  12.5 0.0 copy-done.4
  12.5 0.1 broadcast_in_dim.10
  12.6 0.0 copy-done.5
  12.6 0.1 copy.24
  12.7 0.1 reshape.12
  13.4 0.0 copy-start.1
  13.4 1.1 %copy-done.1 = bf16[1,4,2,192,192]{4,3,2,1,0:T(8,128)(2,1)S(1)} copy-done((bf16[1,4,2,192,192]{4,3,2,1,0:T(8,128)(2,1)S(1)}, bf16[1,4,2,192,192]{4,3,2,1,0:T(8,128)(2,1)}, u32[]{:S(2)}) %copy-start.1) | copy-done | bytes 589848
  14.5 0.0 copy-start.2
  14.5 1.0 copy-done.2
  15.5 0.0 copy-start.3
  15.5 0.3 left.1
  15.8 0.1 pad_add_fusion.meta
  15.9 0.7 copy-done.3
  16.7 0.1 slice_bitcast_fusion.1
  16.7 1.0 %pad_maximum_fusion.table = bf16[4,192,384]{2,1,0:T(8,128)(2,1)} fusion(bf16[4,192,192]{2,1,0:T(8,128)(2,1)S(1)} %get-tuple-element.36, bf16[4,192,192]{2,1,0:T(8,128)(2,1)S(1)} %get-tuple-element.35), kind=kLoop, calls=%fused_computation | loop fusion | flops 1179648 | bytes 1179648 | tf_op jit(solution)/shard_map/concatenate | solution.py:208
  17.8 47.8 %all-to-all-done = bf16[1,16,2,48,768]{4,3,2,0,1:T(8,128)(2,1)S(1)} async-done(((bf16[1,16,2,48,768]{4,3,2,0,1:T(8,128)(2,1)}), bf16[1,16,2,48,768]{4,3,2,0,1:T(8,128)(2,1)S(1)}, u32[]{:S(2)}, u32[]{:S(2)}) %all-to-all-start) | async-done | bytes 2359328 | tf_op jit(solution)/shard_map/all_to_all | solution.py:205
  65.5 0.1 broadcast_in_dim.11.gamma.refs_0_
  65.6 1.9 %dress.1._.block = bf16[2,768,128]{2,1,0:T(8,128)(2,1)S(1)} custom-call(f32[32,128]{1,0:T(8,128)S(1)} %broadcast_in_dim.11.gamma.refs_0_, bf16[1536,768]{1,0:T(8,128)(2,1)S(1)} %bitcast.14, bf16[256,2048]{1,0:T(8,128)(2,1)S(1)} %left.1), custom_call_target="tpu_custom_call" | custom-call | tf_op jit(solution)/shard_map/dress/pallas_call | solution.py:231
  67.5 3.5 %collective-permute-start = (bf16[2,768,128]{2,1,0:T(8,128)(2,1)S(1)}, bf16[2,768,128]{2,1,0:T(8,128)(2,1)S(1)}, u32[]{:S(2)}, u32[]{:S(2)}) collective-permute-start(bf16[2,768,128]{2,1,0:T(8,128)(2,1)S(1)} %dress.1._.block), channel_id=1, source_target_pairs={{0,16},{32,48},{64,80},{96,112},{128,144},{160,176},{192,208},{224... | collective-permute-start | bytes 1179656 | tf_op jit(solution)/shard_map/ppermute | solution.py:19
  71.0 5.4 %collective-permute-start.1 = (bf16[2,768,128]{2,1,0:T(8,128)(2,1)S(1)}, bf16[2,768,128]{2,1,0:T(8,128)(2,1)S(1)}, u32[]{:S(2)}, u32[]{:S(2)}) collective-permute-start(bf16[2,768,128]{2,1,0:T(8,128)(2,1)S(1)} %dress.1._.block), channel_id=1, source_target_pairs={{16,32},{48,64},{80,96},{112,128},{144,160},{176,192},{208,224},{2... | collective-permute-start | bytes 1179656 | tf_op jit(solution)/shard_map/ppermute | solution.py:19
  76.4 2.5 %sort.1.tau.refs_1_ = bf16[1536,768]{1,0:T(8,128)(2,1)S(1)} custom-call(bf16[1536,768]{1,0:T(8,128)(2,1)S(1)} %bitcast.15, bf16[2,768,128]{2,1,0:T(8,128)(2,1)S(1)} %dress.1._.block), custom_call_target="tpu_custom_call", output_to_operand_aliasing={{}: (0, {})} | custom-call | tf_op jit(solution)/shard_map/sort/pallas_call | solution.py:267
  79.0 1.2 %collective-permute-done.refs_2_ = bf16[2,768,128]{2,1,0:T(8,128)(2,1)S(1)} collective-permute-done((bf16[2,768,128]{2,1,0:T(8,128)(2,1)S(1)}, bf16[2,768,128]{2,1,0:T(8,128)(2,1)S(1)}, u32[]{:S(2)}, u32[]{:S(2)}) %collective-permute-start) | collective-permute-done | bytes 393248 | tf_op jit(solution)/shard_map/ppermute | solution.py:19
  80.2 5.6 %collective-permute-start.3 = (bf16[2,768,128]{2,1,0:T(8,128)(2,1)S(1)}, bf16[2,768,128]{2,1,0:T(8,128)(2,1)S(1)}, u32[]{:S(2)}, u32[]{:S(2)}) collective-permute-start(bf16[2,768,128]{2,1,0:T(8,128)(2,1)S(1)} %collective-permute-done.refs_2_), channel_id=1, source_target_pairs={{16,32},{48,64},{80,96},{112,128},{144,160},{176,192},{208,224},{2... | collective-permute-start | bytes 1179656 | tf_op jit(solution)/shard_map/ppermute | solution.py:19
  85.9 0.0 collective-permute-done.1.refs_3_
  85.9 2.1 %collective-permute-start.2 = (bf16[2,768,128]{2,1,0:T(8,128)(2,1)S(1)}, bf16[2,768,128]{2,1,0:T(8,128)(2,1)S(1)}, u32[]{:S(2)}, u32[]{:S(2)}) collective-permute-start(bf16[2,768,128]{2,1,0:T(8,128)(2,1)S(1)} %collective-permute-done.1.refs_3_), channel_id=1, source_target_pairs={{0,16},{32,48},{64,80},{96,112},{128,144},{160,176},{192,208},{224... | collective-permute-start | bytes 1179656 | tf_op jit(solution)/shard_map/ppermute | solution.py:19
  88.0 1.3 %own.1 = (bf16[5,128,1536]{2,1,0:T(8,128)(2,1)S(1)}, bf16[5,384,1024]{2,1,0:T(8,128)(2,1)S(1)}, bf16[4,192,384]{2,1,0:T(8,128)(2,1)S(1)}) custom-call(f32[32,128]{1,0:T(8,128)S(1)} %broadcast_in_dim.11.gamma.refs_0_, bf16[1536,768]{1,0:T(8,128)(2,1)S(1)} %sort.1.tau.refs_1_, bf16[2,768,128]{2,1,0:T(8,128)(2,1)S(1)} %dress.1._.block, ...), custom_call_target="tpu_custom_call" | custom-call | tf_op jit(solution)/shard_map/own/pallas_call | solution.py:280
  89.3 2.4 %prepare.2 = (bf16[5,128,1536]{2,1,0:T(8,128)(2,1)S(1)}, bf16[5,384,1024]{2,1,0:T(8,128)(2,1)S(1)}) custom-call(f32[32,128]{1,0:T(8,128)S(1)} %broadcast_in_dim.11.gamma.refs_0_, bf16[1536,768]{1,0:T(8,128)(2,1)S(1)} %sort.1.tau.refs_1_, bf16[2,768,128]{2,1,0:T(8,128)(2,1)S(1)} %collective-permute-done.refs_2_, ...), custom_call_target="tpu_custom_call", output_to_operand_aliasing={{0}: (4, {}), {1}: (5, {})} | custom-call | tf_op jit(solution)/shard_map/prepare/pallas_call | solution.py:251
  91.7 2.5 %collective-permute-done.3.refs_2_ = bf16[2,768,128]{2,1,0:T(8,128)(2,1)S(1)} collective-permute-done((bf16[2,768,128]{2,1,0:T(8,128)(2,1)S(1)}, bf16[2,768,128]{2,1,0:T(8,128)(2,1)S(1)}, u32[]{:S(2)}, u32[]{:S(2)}) %collective-permute-start.3) | collective-permute-done | bytes 393248 | tf_op jit(solution)/shard_map/ppermute | solution.py:19
  94.2 1.4 %prepare.3 = (bf16[5,128,1536]{2,1,0:T(8,128)(2,1)S(1)}, bf16[5,384,1024]{2,1,0:T(8,128)(2,1)S(1)}) custom-call(f32[32,128]{1,0:T(8,128)S(1)} %broadcast_in_dim.11.gamma.refs_0_, bf16[1536,768]{1,0:T(8,128)(2,1)S(1)} %sort.1.tau.refs_1_, bf16[2,768,128]{2,1,0:T(8,128)(2,1)S(1)} %collective-permute-done.3.refs_2_, ...), custom_call_target="tpu_custom_call", output_to_operand_aliasing={{0}: (3, {}), {1}: (4, {})} | custom-call | tf_op jit(solution)/shard_map/prepare/pallas_call | solution.py:251
  95.5 1.9 %collective-permute-done.2.last = bf16[2,768,128]{2,1,0:T(8,128)(2,1)S(1)} collective-permute-done((bf16[2,768,128]{2,1,0:T(8,128)(2,1)S(1)}, bf16[2,768,128]{2,1,0:T(8,128)(2,1)S(1)}, u32[]{:S(2)}, u32[]{:S(2)}) %collective-permute-start.2) | collective-permute-done | bytes 393248 | tf_op jit(solution)/shard_map/ppermute | solution.py:19
  97.4 5.0 %diagrams.1 = (f32[6,2,128,128]{3,2,1,0:T(8,128)}, bf16[5,128,1536]{2,1,0:T(8,128)(2,1)S(1)}, bf16[5,384,1024]{2,1,0:T(8,128)(2,1)S(1)}) custom-call(s32[20]{0:T(128)S(1)} %pad_add_fusion.meta, f32[32,128]{1,0:T(8,128)S(1)} %broadcast_in_dim.11.gamma.refs_0_, bf16[1536,768]{1,0:T(8,128)(2,1)S(1)} %sort.1.tau.refs_1_, ...), custom_call_target="tpu_custom_call", output_to_operand_aliasing={{1}: (5, {}), {2}: (6, {})} | custom-call | tf_op jit(solution)/shard_map/diagrams/pallas_call | solution.py:291
Async XLA Ops:
  0.0 10.6 %copy-start = (bf16[1,4,2,192,192]{4,3,2,1,0:T(8,128)(2,1)S(1)}, bf16[1,4,2,192,192]{4,3,2,1,0:T(8,128)(2,1)}, u32[]{:S(2)}) copy-start(bf16[1,4,2,192,192]{4,3,2,1,0:T(8,128)(2,1)} %param.8) | copy-start | bytes 1769476
  0.0 12.5 %copy-start.4 = (f32[2,4,4]{2,1,0:T(4,128)S(1)}, f32[2,4,4]{2,1,0:T(4,128)}, u32[]{:S(2)}) copy-start(f32[2,4,4]{2,1,0:T(4,128)} %param.10) | copy-start | bytes 388
  0.0 12.6 %copy-start.5 = (s32[1,6,3]{1,0,2:T(1,128)S(1)}, s32[1,6,3]{1,0,2:T(1,128)}, u32[]{:S(2)}) copy-start(s32[1,6,3]{1,0,2:T(1,128)} %param.11) | copy-start | bytes 220
  0.0 65.5 %all-to-all-start = ((bf16[1,16,2,48,768]{4,3,2,0,1:T(8,128)(2,1)}), bf16[1,16,2,48,768]{4,3,2,0,1:T(8,128)(2,1)S(1)}, u32[]{:S(2)}, u32[]{:S(2)}) async-start(bf16[1,16,2,48,768]{4,3,2,0,1:T(8,128)(2,1)} %bitcast.18), calls=%async_computation | async-start | bytes 4718592 | tf_op jit(solution)/shard_map/all_to_all | solution.py:205
  13.4 1.1 %copy-start.1 = (bf16[1,4,2,192,192]{4,3,2,1,0:T(8,128)(2,1)S(1)}, bf16[1,4,2,192,192]{4,3,2,1,0:T(8,128)(2,1)}, u32[]{:S(2)}) copy-start(bf16[1,4,2,192,192]{4,3,2,1,0:T(8,128)(2,1)} %param.8) | copy-start | bytes 1769476
  14.5 1.0 copy-start.2
  15.5 1.1 %copy-start.3 = (bf16[1,4,2,192,192]{3,4,1,2,0:T(8,128)(2,1)S(1)}, bf16[1,4,2,192,192]{3,4,1,2,0:T(8,128)(2,1)}, u32[]{:S(2)}) copy-start(bf16[1,4,2,192,192]{3,4,1,2,0:T(8,128)(2,1)} %copy.22) | copy-start | bytes 1769476
  67.5 12.7 %collective-permute-start = (bf16[2,768,128]{2,1,0:T(8,128)(2,1)S(1)}, bf16[2,768,128]{2,1,0:T(8,128)(2,1)S(1)}, u32[]{:S(2)}, u32[]{:S(2)}) collective-permute-start(bf16[2,768,128]{2,1,0:T(8,128)(2,1)S(1)} %dress.1._.block), channel_id=1, source_target_pairs={{0,16},{32,48},{64,80},{96,112},{128,144},{160,176},{192,208},{224... | collective-permute-start | bytes 1179656 | tf_op jit(solution)/shard_map/ppermute | solution.py:19
  71.0 14.8 %collective-permute-start.1 = (bf16[2,768,128]{2,1,0:T(8,128)(2,1)S(1)}, bf16[2,768,128]{2,1,0:T(8,128)(2,1)S(1)}, u32[]{:S(2)}, u32[]{:S(2)}) collective-permute-start(bf16[2,768,128]{2,1,0:T(8,128)(2,1)S(1)} %dress.1._.block), channel_id=1, source_target_pairs={{16,32},{48,64},{80,96},{112,128},{144,160},{176,192},{208,224},{2... | collective-permute-start | bytes 1179656 | tf_op jit(solution)/shard_map/ppermute | solution.py:19
  80.2 13.9 %collective-permute-start.3 = (bf16[2,768,128]{2,1,0:T(8,128)(2,1)S(1)}, bf16[2,768,128]{2,1,0:T(8,128)(2,1)S(1)}, u32[]{:S(2)}, u32[]{:S(2)}) collective-permute-start(bf16[2,768,128]{2,1,0:T(8,128)(2,1)S(1)} %collective-permute-done.refs_2_), channel_id=1, source_target_pairs={{16,32},{48,64},{80,96},{112,128},{144,160},{176,192},{208,224},{2... | collective-permute-start | bytes 1179656 | tf_op jit(solution)/shard_map/ppermute | solution.py:19
  85.9 11.6 %collective-permute-start.2 = (bf16[2,768,128]{2,1,0:T(8,128)(2,1)S(1)}, bf16[2,768,128]{2,1,0:T(8,128)(2,1)S(1)}, u32[]{:S(2)}, u32[]{:S(2)}) collective-permute-start(bf16[2,768,128]{2,1,0:T(8,128)(2,1)S(1)} %collective-permute-done.1.refs_3_), channel_id=1, source_target_pairs={{0,16},{32,48},{64,80},{96,112},{128,144},{160,176},{192,208},{224... | collective-permute-start | bytes 1179656 | tf_op jit(solution)/shard_map/ppermute | solution.py:19

commit v5 on v4

--- a/solution.py
+++ b/solution.py
@@ -9,6 +9,7 @@
 
 DT = 2
 TILE = 16
+SURE = 2
 BF = jnp.bfloat16
 F32 = jnp.float32
 
@@ -156,10 +157,20 @@
 ):
     ndim, width = last.shape[1:]
     nev = ndim // 4
-    prepare(3, last, gamma, tau, wide, mixed, rows, split, depth)
+    slots = out.shape[0]
+    count = meta[meta.shape[0] - 2]
+    here = meta[meta.shape[0] - 1]
     scale = (2.0 * ndim) ** (-0.5)
-    here = meta[meta.shape[0] - 1]
     sign = 1 - 2 * (here % 2)
+
+    def store(k):
+        return pltpu.make_async_copy(totals.at[k], out.at[k], sem.at[k])
+
+    @pl.when(count <= SURE)
+    def _():
+        totals[SURE:] = jnp.zeros((slots - SURE, *totals.shape[1:]), F32)
+        for k in range(SURE, slots):
+            store(k).start()
 
     def entry(sender):
         ahead = (sender - here) * sign
@@ -167,15 +178,16 @@
         far = jnp.where(ahead == 2, 3, 4)
         return jnp.where(ahead == 0, 0, jnp.where(ahead * ahead == 1, near, far))
 
-    for k in range(out.shape[0]):
+    def diagram(k):
         first = entry(meta[3 * k])
         second = entry(meta[3 * k + 1])
+        table = backward.at[meta[3 * k + 2]]
         pair = column.at[k % 2]
         for half in range(2):
             at = 2 * half * width
-            real = dot(backward[meta[3 * k + 2]], mixed[first, :, at : at + 2 * width]).astype(BF)
+            real = dot(table[...], mixed[first, :, at : at + 2 * width]).astype(BF)
             at += 4 * width
-            imag = dot(backward[meta[3 * k + 2]], mixed[first, :, at : at + 2 * width]).astype(BF)
+            imag = dot(table[...], mixed[first, :, at : at + 2 * width]).astype(BF)
             for q in range(2):
                 s = 2 * half + q
                 part = slice(q * width, (q + 1) * width)
@@ -186,12 +198,22 @@
                 pair[low, :width] = imag[:, part]
                 pair[low, width:] = -real[:, part]
         result = dot(wide[second], pair[...]) * scale
-        result = jnp.where(k < meta[meta.shape[0] - 2], result, 0.0)
+        result = jnp.where(k < count, result, 0.0)
         totals[k, 0] = result[:, :width]
         totals[k, 1] = result[:, width:]
-        pltpu.make_async_copy(totals.at[k], out.at[k], sem.at[k]).start()
-    for k in range(out.shape[0]):
-        pltpu.make_async_copy(totals.at[k], out.at[k], sem.at[k]).wait()
+        store(k).start()
+
+    prepare(3, last, gamma, tau, wide, mixed, rows, split, depth)
+    for k in range(SURE):
+        diagram(k)
+
+    @pl.when(count > SURE)
+    def _():
+        for k in range(SURE, slots):
+            diagram(k)
+
+    for k in range(slots):
+        store(k).wait()
 
 
 def per_device(

time: 103 us -> 103 us (level); the launches traced: 103 us -> 101 us
  Pallas kernels: 14.8 us -> 13.2 us
    pallas_call x1, Pallas kernels: 5.03 us -> 3.43 us  [per_device(): pl.pallas_call(functools.partial(diagrams_kernel, depth=depth), out_shape...]
where the time goes in v5:
time: 103 us; the launch traced here: 101 us
  waiting for transfers between devices  53.6 us (52%)
  starting transfers between devices  27 us (26%)
  Pallas kernels  13.2 us (13%)
  local copies, waits for them, and re-layouts  4.48 us (4%)
  between operations  1.45 us (1%)
  other arithmetic  1.11 us (1%)
    all_to_all x1, waiting for transfers between devices, per_device(): lax.all_to_all(perambulator, 'col', split_axis=1, concat_axis=1, tiled=True)  47.8 us
    ppermute x4, starting transfers between devices, swapped(): lax.ppermute(shard, axis, [(i, i + 1) for i in lower] + [(i + 1, i) for i...  16.5 us
    all_to_all x1, starting transfers between devices, per_device(): lax.all_to_all(perambulator, 'col', split_axis=1, concat_axis=1, tiled=True)  10.6 us
    ppermute x4, waiting for transfers between devices, swapped(): lax.ppermute(shard, axis, [(i, i + 1) for i in lower] + [(i + 1, i) for i...  5.8 us
    unnamed x14, local copies, waits for them, and re-layouts  4.19 us
    pallas_call x2, Pallas kernels, prepared(): pl.pallas_call(functools.partial(prepare_kernel, depth=depth, entries=ent...  3.74 us
    pallas_call x1, Pallas kernels, per_device(): pl.pallas_call(functools.partial(diagrams_kernel, depth=depth), out_shape...  3.43 us
    pallas_call x1, Pallas kernels, per_device(): pl.pallas_call(sort_kernel, out_shape=jax.ShapeDtypeStruct(tau.shape, BF)...  2.53 us
  transfers between devices with their start and end apart: 5, of which 4 were waited for; matrix products, arithmetic and copies ran while one was open for 3% of the time, Pallas kernels for 8%

profile of v5, /device:TPU:6, one launch (start us, length us, event | category | flops | bytes accessed | tf_op | source)
XLA Modules:
  0.0 100.9 jit_solution(8893791667309201400)
XLA Ops:
  0.0 0.0 copy-start
  0.0 0.0 copy-start.4
  0.0 0.0 copy-start.5
  0.0 10.6 %all-to-all-start = ((bf16[1,16,2,48,768]{4,3,2,0,1:T(8,128)(2,1)}), bf16[1,16,2,48,768]{4,3,2,0,1:T(8,128)(2,1)S(1)}, u32[]{:S(2)}, u32[]{:S(2)}) async-start(bf16[1,16,2,48,768]{4,3,2,0,1:T(8,128)(2,1)} %bitcast.18), calls=%async_computation | async-start | bytes 4718592 | tf_op jit(solution)/shard_map/all_to_all | solution.py:227
  10.6 0.0 copy-done
  10.6 1.2 %copy.22 = bf16[1,4,2,192,192]{3,4,1,2,0:T(8,128)(2,1)} copy(bf16[1,4,2,192,192]{4,3,2,1,0:T(8,128)(2,1)S(1)} %copy-done) | data formatting | bytes 1179648 | tf_op args[1]
  12.5 0.0 copy-done.4
  12.5 0.1 broadcast_in_dim.10
  12.6 0.0 copy-done.5
  12.6 0.1 copy.24
  12.7 0.1 reshape.12
  13.4 0.0 copy-start.1
  13.4 1.1 %copy-done.1 = bf16[1,4,2,192,192]{4,3,2,1,0:T(8,128)(2,1)S(1)} copy-done((bf16[1,4,2,192,192]{4,3,2,1,0:T(8,128)(2,1)S(1)}, bf16[1,4,2,192,192]{4,3,2,1,0:T(8,128)(2,1)}, u32[]{:S(2)}) %copy-start.1) | copy-done | bytes 589848
  14.5 0.0 copy-start.2
  14.5 1.0 copy-done.2
  15.5 0.0 copy-start.3
  15.5 0.3 left.1
  15.8 0.1 pad_add_fusion.meta
  15.9 0.7 copy-done.3
  16.7 0.1 slice_bitcast_fusion.1
  16.7 1.0 %pad_maximum_fusion.table = bf16[4,192,384]{2,1,0:T(8,128)(2,1)} fusion(bf16[4,192,192]{2,1,0:T(8,128)(2,1)S(1)} %get-tuple-element.36, bf16[4,192,192]{2,1,0:T(8,128)(2,1)S(1)} %get-tuple-element.35), kind=kLoop, calls=%fused_computation | loop fusion | flops 1179648 | bytes 1179648 | tf_op jit(solution)/shard_map/concatenate | solution.py:230
  17.8 47.8 %all-to-all-done = bf16[1,16,2,48,768]{4,3,2,0,1:T(8,128)(2,1)S(1)} async-done(((bf16[1,16,2,48,768]{4,3,2,0,1:T(8,128)(2,1)}), bf16[1,16,2,48,768]{4,3,2,0,1:T(8,128)(2,1)S(1)}, u32[]{:S(2)}, u32[]{:S(2)}) %all-to-all-start) | async-done | bytes 2359328 | tf_op jit(solution)/shard_map/all_to_all | solution.py:227
  65.5 0.1 broadcast_in_dim.11.gamma.refs_0_
  65.6 1.9 %dress.1._.block = bf16[2,768,128]{2,1,0:T(8,128)(2,1)S(1)} custom-call(f32[32,128]{1,0:T(8,128)S(1)} %broadcast_in_dim.11.gamma.refs_0_, bf16[1536,768]{1,0:T(8,128)(2,1)S(1)} %bitcast.14, bf16[256,2048]{1,0:T(8,128)(2,1)S(1)} %left.1), custom_call_target="tpu_custom_call" | custom-call | tf_op jit(solution)/shard_map/dress/pallas_call | solution.py:253
  67.5 3.5 %collective-permute-start = (bf16[2,768,128]{2,1,0:T(8,128)(2,1)S(1)}, bf16[2,768,128]{2,1,0:T(8,128)(2,1)S(1)}, u32[]{:S(2)}, u32[]{:S(2)}) collective-permute-start(bf16[2,768,128]{2,1,0:T(8,128)(2,1)S(1)} %dress.1._.block), channel_id=1, source_target_pairs={{0,16},{32,48},{64,80},{96,112},{128,144},{160,176},{192,208},{224... | collective-permute-start | bytes 1179656 | tf_op jit(solution)/shard_map/ppermute | solution.py:20
  71.0 5.4 %collective-permute-start.1 = (bf16[2,768,128]{2,1,0:T(8,128)(2,1)S(1)}, bf16[2,768,128]{2,1,0:T(8,128)(2,1)S(1)}, u32[]{:S(2)}, u32[]{:S(2)}) collective-permute-start(bf16[2,768,128]{2,1,0:T(8,128)(2,1)S(1)} %dress.1._.block), channel_id=1, source_target_pairs={{16,32},{48,64},{80,96},{112,128},{144,160},{176,192},{208,224},{2... | collective-permute-start | bytes 1179656 | tf_op jit(solution)/shard_map/ppermute | solution.py:20
  76.4 2.5 %sort.1.tau.refs_1_ = bf16[1536,768]{1,0:T(8,128)(2,1)S(1)} custom-call(bf16[1536,768]{1,0:T(8,128)(2,1)S(1)} %bitcast.15, bf16[2,768,128]{2,1,0:T(8,128)(2,1)S(1)} %dress.1._.block), custom_call_target="tpu_custom_call", output_to_operand_aliasing={{}: (0, {})} | custom-call | tf_op jit(solution)/shard_map/sort/pallas_call | solution.py:289
  79.0 1.2 %collective-permute-done.refs_2_ = bf16[2,768,128]{2,1,0:T(8,128)(2,1)S(1)} collective-permute-done((bf16[2,768,128]{2,1,0:T(8,128)(2,1)S(1)}, bf16[2,768,128]{2,1,0:T(8,128)(2,1)S(1)}, u32[]{:S(2)}, u32[]{:S(2)}) %collective-permute-start) | collective-permute-done | bytes 393248 | tf_op jit(solution)/shard_map/ppermute | solution.py:20
  80.2 5.6 %collective-permute-start.3 = (bf16[2,768,128]{2,1,0:T(8,128)(2,1)S(1)}, bf16[2,768,128]{2,1,0:T(8,128)(2,1)S(1)}, u32[]{:S(2)}, u32[]{:S(2)}) collective-permute-start(bf16[2,768,128]{2,1,0:T(8,128)(2,1)S(1)} %collective-permute-done.refs_2_), channel_id=1, source_target_pairs={{16,32},{48,64},{80,96},{112,128},{144,160},{176,192},{208,224},{2... | collective-permute-start | bytes 1179656 | tf_op jit(solution)/shard_map/ppermute | solution.py:20
  85.9 0.0 collective-permute-done.1.refs_3_
  85.9 1.9 %collective-permute-start.2 = (bf16[2,768,128]{2,1,0:T(8,128)(2,1)S(1)}, bf16[2,768,128]{2,1,0:T(8,128)(2,1)S(1)}, u32[]{:S(2)}, u32[]{:S(2)}) collective-permute-start(bf16[2,768,128]{2,1,0:T(8,128)(2,1)S(1)} %collective-permute-done.1.refs_3_), channel_id=1, source_target_pairs={{0,16},{32,48},{64,80},{96,112},{128,144},{160,176},{192,208},{224... | collective-permute-start | bytes 1179656 | tf_op jit(solution)/shard_map/ppermute | solution.py:20
  87.8 1.3 %own.1 = (bf16[5,128,1536]{2,1,0:T(8,128)(2,1)S(1)}, bf16[5,384,1024]{2,1,0:T(8,128)(2,1)S(1)}, bf16[4,192,384]{2,1,0:T(8,128)(2,1)S(1)}) custom-call(f32[32,128]{1,0:T(8,128)S(1)} %broadcast_in_dim.11.gamma.refs_0_, bf16[1536,768]{1,0:T(8,128)(2,1)S(1)} %sort.1.tau.refs_1_, bf16[2,768,128]{2,1,0:T(8,128)(2,1)S(1)} %dress.1._.block, ...), custom_call_target="tpu_custom_call" | custom-call | tf_op jit(solution)/shard_map/own/pallas_call | solution.py:302
  89.1 2.4 %prepare.2 = (bf16[5,128,1536]{2,1,0:T(8,128)(2,1)S(1)}, bf16[5,384,1024]{2,1,0:T(8,128)(2,1)S(1)}) custom-call(f32[32,128]{1,0:T(8,128)S(1)} %broadcast_in_dim.11.gamma.refs_0_, bf16[1536,768]{1,0:T(8,128)(2,1)S(1)} %sort.1.tau.refs_1_, bf16[2,768,128]{2,1,0:T(8,128)(2,1)S(1)} %collective-permute-done.refs_2_, ...), custom_call_target="tpu_custom_call", output_to_operand_aliasing={{0}: (4, {}), {1}: (5, {})} | custom-call | tf_op jit(solution)/shard_map/prepare/pallas_call | solution.py:273
  91.5 2.7 %collective-permute-done.3.refs_2_ = bf16[2,768,128]{2,1,0:T(8,128)(2,1)S(1)} collective-permute-done((bf16[2,768,128]{2,1,0:T(8,128)(2,1)S(1)}, bf16[2,768,128]{2,1,0:T(8,128)(2,1)S(1)}, u32[]{:S(2)}, u32[]{:S(2)}) %collective-permute-start.3) | collective-permute-done | bytes 393248 | tf_op jit(solution)/shard_map/ppermute | solution.py:20
  94.2 1.4 %prepare.3 = (bf16[5,128,1536]{2,1,0:T(8,128)(2,1)S(1)}, bf16[5,384,1024]{2,1,0:T(8,128)(2,1)S(1)}) custom-call(f32[32,128]{1,0:T(8,128)S(1)} %broadcast_in_dim.11.gamma.refs_0_, bf16[1536,768]{1,0:T(8,128)(2,1)S(1)} %sort.1.tau.refs_1_, bf16[2,768,128]{2,1,0:T(8,128)(2,1)S(1)} %collective-permute-done.3.refs_2_, ...), custom_call_target="tpu_custom_call", output_to_operand_aliasing={{0}: (3, {}), {1}: (4, {})} | custom-call | tf_op jit(solution)/shard_map/prepare/pallas_call | solution.py:273
  95.5 1.9 %collective-permute-done.2.last = bf16[2,768,128]{2,1,0:T(8,128)(2,1)S(1)} collective-permute-done((bf16[2,768,128]{2,1,0:T(8,128)(2,1)S(1)}, bf16[2,768,128]{2,1,0:T(8,128)(2,1)S(1)}, u32[]{:S(2)}, u32[]{:S(2)}) %collective-permute-start.2) | collective-permute-done | bytes 393248 | tf_op jit(solution)/shard_map/ppermute | solution.py:20
  97.4 3.4 %diagrams.1 = (f32[6,2,128,128]{3,2,1,0:T(8,128)}, bf16[5,128,1536]{2,1,0:T(8,128)(2,1)S(1)}, bf16[5,384,1024]{2,1,0:T(8,128)(2,1)S(1)}) custom-call(s32[20]{0:T(128)S(1)} %pad_add_fusion.meta, f32[32,128]{1,0:T(8,128)S(1)} %broadcast_in_dim.11.gamma.refs_0_, bf16[1536,768]{1,0:T(8,128)(2,1)S(1)} %sort.1.tau.refs_1_, ...), custom_call_target="tpu_custom_call", output_to_operand_aliasing={{1}: (5, {}), {2}: (6, {})} | custom-call | tf_op jit(solution)/shard_map/diagrams/pallas_call | solution.py:313
Async XLA Ops:
  0.0 10.6 %copy-start = (bf16[1,4,2,192,192]{4,3,2,1,0:T(8,128)(2,1)S(1)}, bf16[1,4,2,192,192]{4,3,2,1,0:T(8,128)(2,1)}, u32[]{:S(2)}) copy-start(bf16[1,4,2,192,192]{4,3,2,1,0:T(8,128)(2,1)} %param.8) | copy-start | bytes 1769476
  0.0 12.5 %copy-start.4 = (f32[2,4,4]{2,1,0:T(4,128)S(1)}, f32[2,4,4]{2,1,0:T(4,128)}, u32[]{:S(2)}) copy-start(f32[2,4,4]{2,1,0:T(4,128)} %param.10) | copy-start | bytes 388
  0.0 12.6 %copy-start.5 = (s32[1,6,3]{1,0,2:T(1,128)S(1)}, s32[1,6,3]{1,0,2:T(1,128)}, u32[]{:S(2)}) copy-start(s32[1,6,3]{1,0,2:T(1,128)} %param.11) | copy-start | bytes 220
  0.0 65.5 %all-to-all-start = ((bf16[1,16,2,48,768]{4,3,2,0,1:T(8,128)(2,1)}), bf16[1,16,2,48,768]{4,3,2,0,1:T(8,128)(2,1)S(1)}, u32[]{:S(2)}, u32[]{:S(2)}) async-start(bf16[1,16,2,48,768]{4,3,2,0,1:T(8,128)(2,1)} %bitcast.18), calls=%async_computation | async-start | bytes 4718592 | tf_op jit(solution)/shard_map/all_to_all | solution.py:227
  13.4 1.1 %copy-start.1 = (bf16[1,4,2,192,192]{4,3,2,1,0:T(8,128)(2,1)S(1)}, bf16[1,4,2,192,192]{4,3,2,1,0:T(8,128)(2,1)}, u32[]{:S(2)}) copy-start(bf16[1,4,2,192,192]{4,3,2,1,0:T(8,128)(2,1)} %param.8) | copy-start | bytes 1769476
  14.5 1.0 copy-start.2
  15.5 1.1 %copy-start.3 = (bf16[1,4,2,192,192]{3,4,1,2,0:T(8,128)(2,1)S(1)}, bf16[1,4,2,192,192]{3,4,1,2,0:T(8,128)(2,1)}, u32[]{:S(2)}) copy-start(bf16[1,4,2,192,192]{3,4,1,2,0:T(8,128)(2,1)} %copy.22) | copy-start | bytes 1769476
  67.5 12.7 %collective-permute-start = (bf16[2,768,128]{2,1,0:T(8,128)(2,1)S(1)}, bf16[2,768,128]{2,1,0:T(8,128)(2,1)S(1)}, u32[]{:S(2)}, u32[]{:S(2)}) collective-permute-start(bf16[2,768,128]{2,1,0:T(8,128)(2,1)S(1)} %dress.1._.block), channel_id=1, source_target_pairs={{0,16},{32,48},{64,80},{96,112},{128,144},{160,176},{192,208},{224... | collective-permute-start | bytes 1179656 | tf_op jit(solution)/shard_map/ppermute | solution.py:20
  71.0 14.8 %collective-permute-start.1 = (bf16[2,768,128]{2,1,0:T(8,128)(2,1)S(1)}, bf16[2,768,128]{2,1,0:T(8,128)(2,1)S(1)}, u32[]{:S(2)}, u32[]{:S(2)}) collective-permute-start(bf16[2,768,128]{2,1,0:T(8,128)(2,1)S(1)} %dress.1._.block), channel_id=1, source_target_pairs={{16,32},{48,64},{80,96},{112,128},{144,160},{176,192},{208,224},{2... | collective-permute-start | bytes 1179656 | tf_op jit(solution)/shard_map/ppermute | solution.py:20
  80.2 13.9 %collective-permute-start.3 = (bf16[2,768,128]{2,1,0:T(8,128)(2,1)S(1)}, bf16[2,768,128]{2,1,0:T(8,128)(2,1)S(1)}, u32[]{:S(2)}, u32[]{:S(2)}) collective-permute-start(bf16[2,768,128]{2,1,0:T(8,128)(2,1)S(1)} %collective-permute-done.refs_2_), channel_id=1, source_target_pairs={{16,32},{48,64},{80,96},{112,128},{144,160},{176,192},{208,224},{2... | collective-permute-start | bytes 1179656 | tf_op jit(solution)/shard_map/ppermute | solution.py:20
  85.9 11.6 %collective-permute-start.2 = (bf16[2,768,128]{2,1,0:T(8,128)(2,1)S(1)}, bf16[2,768,128]{2,1,0:T(8,128)(2,1)S(1)}, u32[]{:S(2)}, u32[]{:S(2)}) collective-permute-start(bf16[2,768,128]{2,1,0:T(8,128)(2,1)S(1)} %collective-permute-done.1.refs_3_), channel_id=1, source_target_pairs={{0,16},{32,48},{64,80},{96,112},{128,144},{160,176},{192,208},{224... | collective-permute-start | bytes 1179656 | tf_op jit(solution)/shard_map/ppermute | solution.py:20

commit v6 on v5

--- a/solution.py
+++ b/solution.py
@@ -66,6 +66,7 @@
     nev = table.shape[3]
     stack_rows(sink[0], sink[1], rows, depth)
     left[:, : rows.shape[0]] = rows[...].T
+    left[:, rows.shape[0] :] = jnp.zeros((left.shape[0], left.shape[1] - rows.shape[0]), BF)
     for c in range(2):
         at = rows.shape[0] + c * 256
         left[:nev, at : at + nev] = table[ident[0], c]
@@ -115,10 +116,11 @@
         mixed[d, low, at_r] = imag.astype(BF)
         mixed[d, low, at_i] = (-real).astype(BF)
 
-    spin_mix(split, gamma, True, write, range(0, nev, TILE))
     stack_rows(block[0], block[1], rows, depth)
     left = rows[...].T
-    for at in range(0, ndim, 2 * width):
+    share = nev // (ndim // (2 * width))
+    for turn, at in enumerate(range(0, ndim, 2 * width)):
+        spin_mix(split, gamma, True, write, range(turn * share, (turn + 1) * share, TILE))
         product = dot(left, tau[:, at : at + 2 * width]).astype(BF)
         wide[d, :, at : at + 2 * width] = product[:width]
         wide[d, :, ndim + at : ndim + at + 2 * width] = product[width:]

time: 103 us -> 103 us (level)
  transfers between devices with their start and end apart: 5 -> 5, of which waited for: 4 -> 4; matrix products, arithmetic and copies ran while one was open for 3% -> 3% of each run, Pallas kernels for 8% -> 7%
where the time goes in v6:
time: 103 us; the launch traced here: 101 us
  waiting for transfers between devices  54 us (52%)
  starting transfers between devices  27 us (26%)
  Pallas kernels  12.8 us (12%)
  local copies, waits for them, and re-layouts  4.47 us (4%)
  between operations  1.45 us (1%)
  other arithmetic  1.11 us (1%)
    all_to_all x1, waiting for transfers between devices, per_device(): lax.all_to_all(perambulator, 'col', split_axis=1, concat_axis=1, tiled=True)  47.8 us
    ppermute x4, starting transfers between devices, swapped(): lax.ppermute(shard, axis, [(i, i + 1) for i in lower] + [(i + 1, i) for i...  16.5 us
    all_to_all x1, starting transfers between devices, per_device(): lax.all_to_all(perambulator, 'col', split_axis=1, concat_axis=1, tiled=True)  10.6 us
    ppermute x4, waiting for transfers between devices, swapped(): lax.ppermute(shard, axis, [(i, i + 1) for i in lower] + [(i + 1, i) for i...  6.25 us
    unnamed x14, local copies, waits for them, and re-layouts  4.18 us
    pallas_call x1, Pallas kernels, per_device(): pl.pallas_call(functools.partial(diagrams_kernel, depth=depth), out_shape...  3.43 us
    pallas_call x2, Pallas kernels, prepared(): pl.pallas_call(functools.partial(prepare_kernel, depth=depth, entries=ent...  3.3 us
    pallas_call x1, Pallas kernels, per_device(): pl.pallas_call(sort_kernel, out_shape=jax.ShapeDtypeStruct(tau.shape, BF)...  2.53 us
  transfers between devices with their start and end apart: 5, of which 4 were waited for; matrix products, arithmetic and copies ran while one was open for 3% of the time, Pallas kernels for 7%

profile of v6, /device:TPU:6, one launch (start us, length us, event | category | flops | bytes accessed | tf_op | source)
XLA Modules:
  0.0 100.9 jit_solution(2276893025331429041)
XLA Ops:
  0.0 0.0 copy-start
  0.0 0.0 copy-start.4
  0.0 0.0 copy-start.5
  0.0 10.6 %all-to-all-start = ((bf16[1,16,2,48,768]{4,3,2,0,1:T(8,128)(2,1)}), bf16[1,16,2,48,768]{4,3,2,0,1:T(8,128)(2,1)S(1)}, u32[]{:S(2)}, u32[]{:S(2)}) async-start(bf16[1,16,2,48,768]{4,3,2,0,1:T(8,128)(2,1)} %bitcast.18), calls=%async_computation | async-start | bytes 4718592 | tf_op jit(solution)/shard_map/all_to_all | solution.py:229
  10.6 0.0 copy-done
  10.6 1.2 %copy.22 = bf16[1,4,2,192,192]{3,4,1,2,0:T(8,128)(2,1)} copy(bf16[1,4,2,192,192]{4,3,2,1,0:T(8,128)(2,1)S(1)} %copy-done) | data formatting | bytes 1179648 | tf_op args[1]
  12.5 0.0 copy-done.4
  12.5 0.1 broadcast_in_dim.10
  12.6 0.0 copy-done.5
  12.6 0.1 copy.24
  12.7 0.1 reshape.12
  13.4 0.0 copy-start.1
  13.4 1.1 %copy-done.1 = bf16[1,4,2,192,192]{4,3,2,1,0:T(8,128)(2,1)S(1)} copy-done((bf16[1,4,2,192,192]{4,3,2,1,0:T(8,128)(2,1)S(1)}, bf16[1,4,2,192,192]{4,3,2,1,0:T(8,128)(2,1)}, u32[]{:S(2)}) %copy-start.1) | copy-done | bytes 589848
  14.5 0.0 copy-start.2
  14.5 1.0 copy-done.2
  15.5 0.0 copy-start.3
  15.5 0.3 left.1
  15.9 0.1 pad_add_fusion.meta
  15.9 0.7 copy-done.3
  16.7 0.1 slice_bitcast_fusion.1
  16.7 1.0 %pad_maximum_fusion.table = bf16[4,192,384]{2,1,0:T(8,128)(2,1)} fusion(bf16[4,192,192]{2,1,0:T(8,128)(2,1)S(1)} %get-tuple-element.36, bf16[4,192,192]{2,1,0:T(8,128)(2,1)S(1)} %get-tuple-element.35), kind=kLoop, calls=%fused_computation | loop fusion | flops 1179648 | bytes 1179648 | tf_op jit(solution)/shard_map/concatenate | solution.py:232
  17.8 47.8 %all-to-all-done = bf16[1,16,2,48,768]{4,3,2,0,1:T(8,128)(2,1)S(1)} async-done(((bf16[1,16,2,48,768]{4,3,2,0,1:T(8,128)(2,1)}), bf16[1,16,2,48,768]{4,3,2,0,1:T(8,128)(2,1)S(1)}, u32[]{:S(2)}, u32[]{:S(2)}) %all-to-all-start) | async-done | bytes 2359328 | tf_op jit(solution)/shard_map/all_to_all | solution.py:229
  65.5 0.1 broadcast_in_dim.11.gamma.refs_0_
  65.6 1.9 %dress.1._.block = bf16[2,768,128]{2,1,0:T(8,128)(2,1)S(1)} custom-call(f32[32,128]{1,0:T(8,128)S(1)} %broadcast_in_dim.11.gamma.refs_0_, bf16[1536,768]{1,0:T(8,128)(2,1)S(1)} %bitcast.14, bf16[256,2048]{1,0:T(8,128)(2,1)S(1)} %left.1), custom_call_target="tpu_custom_call" | custom-call | tf_op jit(solution)/shard_map/dress/pallas_call | solution.py:255
  67.5 3.5 %collective-permute-start = (bf16[2,768,128]{2,1,0:T(8,128)(2,1)S(1)}, bf16[2,768,128]{2,1,0:T(8,128)(2,1)S(1)}, u32[]{:S(2)}, u32[]{:S(2)}) collective-permute-start(bf16[2,768,128]{2,1,0:T(8,128)(2,1)S(1)} %dress.1._.block), channel_id=1, source_target_pairs={{0,16},{32,48},{64,80},{96,112},{128,144},{160,176},{192,208},{224... | collective-permute-start | bytes 1179656 | tf_op jit(solution)/shard_map/ppermute | solution.py:20
  71.0 5.4 %collective-permute-start.1 = (bf16[2,768,128]{2,1,0:T(8,128)(2,1)S(1)}, bf16[2,768,128]{2,1,0:T(8,128)(2,1)S(1)}, u32[]{:S(2)}, u32[]{:S(2)}) collective-permute-start(bf16[2,768,128]{2,1,0:T(8,128)(2,1)S(1)} %dress.1._.block), channel_id=1, source_target_pairs={{16,32},{48,64},{80,96},{112,128},{144,160},{176,192},{208,224},{2... | collective-permute-start | bytes 1179656 | tf_op jit(solution)/shard_map/ppermute | solution.py:20
  76.4 2.5 %sort.1.tau.refs_1_ = bf16[1536,768]{1,0:T(8,128)(2,1)S(1)} custom-call(bf16[1536,768]{1,0:T(8,128)(2,1)S(1)} %bitcast.15, bf16[2,768,128]{2,1,0:T(8,128)(2,1)S(1)} %dress.1._.block), custom_call_target="tpu_custom_call", output_to_operand_aliasing={{}: (0, {})} | custom-call | tf_op jit(solution)/shard_map/sort/pallas_call | solution.py:291
  79.0 1.2 %collective-permute-done.refs_2_ = bf16[2,768,128]{2,1,0:T(8,128)(2,1)S(1)} collective-permute-done((bf16[2,768,128]{2,1,0:T(8,128)(2,1)S(1)}, bf16[2,768,128]{2,1,0:T(8,128)(2,1)S(1)}, u32[]{:S(2)}, u32[]{:S(2)}) %collective-permute-start) | collective-permute-done | bytes 393248 | tf_op jit(solution)/shard_map/ppermute | solution.py:20
  80.2 5.6 %collective-permute-start.3 = (bf16[2,768,128]{2,1,0:T(8,128)(2,1)S(1)}, bf16[2,768,128]{2,1,0:T(8,128)(2,1)S(1)}, u32[]{:S(2)}, u32[]{:S(2)}) collective-permute-start(bf16[2,768,128]{2,1,0:T(8,128)(2,1)S(1)} %collective-permute-done.refs_2_), channel_id=1, source_target_pairs={{16,32},{48,64},{80,96},{112,128},{144,160},{176,192},{208,224},{2... | collective-permute-start | bytes 1179656 | tf_op jit(solution)/shard_map/ppermute | solution.py:20
  85.9 0.0 collective-permute-done.1.refs_3_
  85.9 1.9 %collective-permute-start.2 = (bf16[2,768,128]{2,1,0:T(8,128)(2,1)S(1)}, bf16[2,768,128]{2,1,0:T(8,128)(2,1)S(1)}, u32[]{:S(2)}, u32[]{:S(2)}) collective-permute-start(bf16[2,768,128]{2,1,0:T(8,128)(2,1)S(1)} %collective-permute-done.1.refs_3_), channel_id=1, source_target_pairs={{0,16},{32,48},{64,80},{96,112},{128,144},{160,176},{192,208},{224... | collective-permute-start | bytes 1179656 | tf_op jit(solution)/shard_map/ppermute | solution.py:20
  87.8 1.3 %own.1 = (bf16[5,128,1536]{2,1,0:T(8,128)(2,1)S(1)}, bf16[5,384,1024]{2,1,0:T(8,128)(2,1)S(1)}, bf16[4,192,384]{2,1,0:T(8,128)(2,1)S(1)}) custom-call(f32[32,128]{1,0:T(8,128)S(1)} %broadcast_in_dim.11.gamma.refs_0_, bf16[1536,768]{1,0:T(8,128)(2,1)S(1)} %sort.1.tau.refs_1_, bf16[2,768,128]{2,1,0:T(8,128)(2,1)S(1)} %dress.1._.block, ...), custom_call_target="tpu_custom_call" | custom-call | tf_op jit(solution)/shard_map/own/pallas_call | solution.py:304
  89.1 2.1 %prepare.2 = (bf16[5,128,1536]{2,1,0:T(8,128)(2,1)S(1)}, bf16[5,384,1024]{2,1,0:T(8,128)(2,1)S(1)}) custom-call(f32[32,128]{1,0:T(8,128)S(1)} %broadcast_in_dim.11.gamma.refs_0_, bf16[1536,768]{1,0:T(8,128)(2,1)S(1)} %sort.1.tau.refs_1_, bf16[2,768,128]{2,1,0:T(8,128)(2,1)S(1)} %collective-permute-done.refs_2_, ...), custom_call_target="tpu_custom_call", output_to_operand_aliasing={{0}: (4, {}), {1}: (5, {})} | custom-call | tf_op jit(solution)/shard_map/prepare/pallas_call | solution.py:275
  91.3 2.9 %collective-permute-done.3.refs_2_ = bf16[2,768,128]{2,1,0:T(8,128)(2,1)S(1)} collective-permute-done((bf16[2,768,128]{2,1,0:T(8,128)(2,1)S(1)}, bf16[2,768,128]{2,1,0:T(8,128)(2,1)S(1)}, u32[]{:S(2)}, u32[]{:S(2)}) %collective-permute-start.3) | collective-permute-done | bytes 393248 | tf_op jit(solution)/shard_map/ppermute | solution.py:20
  94.2 1.2 %prepare.3 = (bf16[5,128,1536]{2,1,0:T(8,128)(2,1)S(1)}, bf16[5,384,1024]{2,1,0:T(8,128)(2,1)S(1)}) custom-call(f32[32,128]{1,0:T(8,128)S(1)} %broadcast_in_dim.11.gamma.refs_0_, bf16[1536,768]{1,0:T(8,128)(2,1)S(1)} %sort.1.tau.refs_1_, bf16[2,768,128]{2,1,0:T(8,128)(2,1)S(1)} %collective-permute-done.3.refs_2_, ...), custom_call_target="tpu_custom_call", output_to_operand_aliasing={{0}: (3, {}), {1}: (4, {})} | custom-call | tf_op jit(solution)/shard_map/prepare/pallas_call | solution.py:275
  95.3 2.1 %collective-permute-done.2.last = bf16[2,768,128]{2,1,0:T(8,128)(2,1)S(1)} collective-permute-done((bf16[2,768,128]{2,1,0:T(8,128)(2,1)S(1)}, bf16[2,768,128]{2,1,0:T(8,128)(2,1)S(1)}, u32[]{:S(2)}, u32[]{:S(2)}) %collective-permute-start.2) | collective-permute-done | bytes 393248 | tf_op jit(solution)/shard_map/ppermute | solution.py:20
  97.4 3.4 %diagrams.1 = (f32[6,2,128,128]{3,2,1,0:T(8,128)}, bf16[5,128,1536]{2,1,0:T(8,128)(2,1)S(1)}, bf16[5,384,1024]{2,1,0:T(8,128)(2,1)S(1)}) custom-call(s32[20]{0:T(128)S(1)} %pad_add_fusion.meta, f32[32,128]{1,0:T(8,128)S(1)} %broadcast_in_dim.11.gamma.refs_0_, bf16[1536,768]{1,0:T(8,128)(2,1)S(1)} %sort.1.tau.refs_1_, ...), custom_call_target="tpu_custom_call", output_to_operand_aliasing={{1}: (5, {}), {2}: (6, {})} | custom-call | tf_op jit(solution)/shard_map/diagrams/pallas_call | solution.py:315
Async XLA Ops:
  0.0 10.6 %copy-start = (bf16[1,4,2,192,192]{4,3,2,1,0:T(8,128)(2,1)S(1)}, bf16[1,4,2,192,192]{4,3,2,1,0:T(8,128)(2,1)}, u32[]{:S(2)}) copy-start(bf16[1,4,2,192,192]{4,3,2,1,0:T(8,128)(2,1)} %param.8) | copy-start | bytes 1769476
  0.0 12.5 %copy-start.4 = (f32[2,4,4]{2,1,0:T(4,128)S(1)}, f32[2,4,4]{2,1,0:T(4,128)}, u32[]{:S(2)}) copy-start(f32[2,4,4]{2,1,0:T(4,128)} %param.10) | copy-start | bytes 388
  0.0 12.6 %copy-start.5 = (s32[1,6,3]{1,0,2:T(1,128)S(1)}, s32[1,6,3]{1,0,2:T(1,128)}, u32[]{:S(2)}) copy-start(s32[1,6,3]{1,0,2:T(1,128)} %param.11) | copy-start | bytes 220
  0.0 65.5 %all-to-all-start = ((bf16[1,16,2,48,768]{4,3,2,0,1:T(8,128)(2,1)}), bf16[1,16,2,48,768]{4,3,2,0,1:T(8,128)(2,1)S(1)}, u32[]{:S(2)}, u32[]{:S(2)}) async-start(bf16[1,16,2,48,768]{4,3,2,0,1:T(8,128)(2,1)} %bitcast.18), calls=%async_computation | async-start | bytes 4718592 | tf_op jit(solution)/shard_map/all_to_all | solution.py:229
  13.4 1.1 %copy-start.1 = (bf16[1,4,2,192,192]{4,3,2,1,0:T(8,128)(2,1)S(1)}, bf16[1,4,2,192,192]{4,3,2,1,0:T(8,128)(2,1)}, u32[]{:S(2)}) copy-start(bf16[1,4,2,192,192]{4,3,2,1,0:T(8,128)(2,1)} %param.8) | copy-start | bytes 1769476
  14.5 1.0 copy-start.2
  15.5 1.1 %copy-start.3 = (bf16[1,4,2,192,192]{3,4,1,2,0:T(8,128)(2,1)S(1)}, bf16[1,4,2,192,192]{3,4,1,2,0:T(8,128)(2,1)}, u32[]{:S(2)}) copy-start(bf16[1,4,2,192,192]{3,4,1,2,0:T(8,128)(2,1)} %copy.22) | copy-start | bytes 1769476
  67.5 12.7 %collective-permute-start = (bf16[2,768,128]{2,1,0:T(8,128)(2,1)S(1)}, bf16[2,768,128]{2,1,0:T(8,128)(2,1)S(1)}, u32[]{:S(2)}, u32[]{:S(2)}) collective-permute-start(bf16[2,768,128]{2,1,0:T(8,128)(2,1)S(1)} %dress.1._.block), channel_id=1, source_target_pairs={{0,16},{32,48},{64,80},{96,112},{128,144},{160,176},{192,208},{224... | collective-permute-start | bytes 1179656 | tf_op jit(solution)/shard_map/ppermute | solution.py:20
  71.0 14.8 %collective-permute-start.1 = (bf16[2,768,128]{2,1,0:T(8,128)(2,1)S(1)}, bf16[2,768,128]{2,1,0:T(8,128)(2,1)S(1)}, u32[]{:S(2)}, u32[]{:S(2)}) collective-permute-start(bf16[2,768,128]{2,1,0:T(8,128)(2,1)S(1)} %dress.1._.block), channel_id=1, source_target_pairs={{16,32},{48,64},{80,96},{112,128},{144,160},{176,192},{208,224},{2... | collective-permute-start | bytes 1179656 | tf_op jit(solution)/shard_map/ppermute | solution.py:20
  80.2 13.9 %collective-permute-start.3 = (bf16[2,768,128]{2,1,0:T(8,128)(2,1)S(1)}, bf16[2,768,128]{2,1,0:T(8,128)(2,1)S(1)}, u32[]{:S(2)}, u32[]{:S(2)}) collective-permute-start(bf16[2,768,128]{2,1,0:T(8,128)(2,1)S(1)} %collective-permute-done.refs_2_), channel_id=1, source_target_pairs={{16,32},{48,64},{80,96},{112,128},{144,160},{176,192},{208,224},{2... | collective-permute-start | bytes 1179656 | tf_op jit(solution)/shard_map/ppermute | solution.py:20
  85.9 11.6 %collective-permute-start.2 = (bf16[2,768,128]{2,1,0:T(8,128)(2,1)S(1)}, bf16[2,768,128]{2,1,0:T(8,128)(2,1)S(1)}, u32[]{:S(2)}, u32[]{:S(2)}) collective-permute-start(bf16[2,768,128]{2,1,0:T(8,128)(2,1)S(1)} %collective-permute-done.1.refs_3_), channel_id=1, source_target_pairs={{0,16},{32,48},{64,80},{96,112},{128,144},{160,176},{192,208},{224... | collective-permute-start | bytes 1179656 | tf_op jit(solution)/shard_map/ppermute | solution.py:20
